TPU v7x, 32 devices: a whole 2x2x4 slice. The times are simulated.
32 devices in a mesh: gx: 8 (over z, x), gy: 4 (over y, core).
Axes of the slice: x: 2, y: 2, z: 4, core: 2. Of those that a mesh axis runs over, the one named last changes fastest.
Arguments:
- self_blk: float32 [64, 128, 128], P(('gx', 'gy')), may hold values from -6 to 6
- near: bfloat16 [64, 14, 512, 128], P(('gx', 'gy')), may hold values from -0.59765625 to 0.59765625
- back: bfloat16 [64, 14, 128, 512], P(('gx', 'gy')), may hold values from -0.59765625 to 0.59765625
- interp: bfloat16 [64, 128, 512], P(('gx', 'gy')), may hold values from -0.59765625 to 0.59765625
- redinv: bfloat16 [64, 512, 512], P(('gx', 'gy')), as said below
- ranks: int32 [64], P(('gx', 'gy')), may hold values from 64 to 128, as said below
- pivots: int32 [64, 128], P(('gx', 'gy')), may hold values from 0 to 511, as said below
- neighbors: int32 [64, 14], P(('gx', 'gy')), may hold values from 0 to 63, as said below
- parent: int32 [64], P(('gx', 'gy')), may hold values from 0 to 63, as said below
Outputs:
- parent_blocks: float32 [64, 128, 128], P(('gx', 'gy'))
Inputs may be any that keep to these rules, and one draw needn't show every extreme that they name: redinv is used only on a box's redundant points. `ranks`: every draw has a box of rank 128 and a box of rank 64. `pivots`: the 128 entries of a box are distinct; the first ranks[b] of them are its skeleton points, the others are redundant points. `neighbors`: box b lies on the device of linear index b // 2, gx major. A box's neighbours are distinct, never the box itself, and lie on devices of the same gy index. The entries of the 2 boxes of one device name boxes of any one device at most 4 times; in every draw and every gy index one device is named exactly 4 times by each other device of that gy index. `parent`: A permutation of the boxes that maps the 8 boxes of each gx index onto the same 8 rows.
All inputs are finite; a program needn't handle non-finite values.
Results may differ from a plain program's by a relative error of at most 0.0049.
Values may be sent and summed in bfloat16 or wider, within the bound.
No kernel may reach another device: no remote copies, remote signals or barrier semaphores. Data moves between devices by JAX's collectives and lax.ppermute only.
A program may use at most 64 MiB of HBM per device.

v0:
```python
import jax
import jax.numpy as jnp
from jax import lax
from jax.sharding import PartitionSpec as P


def box_terms(near_b, back_b, interp_b, redinv_b, rank_b, pivot_b):
    points_count = redinv_b.shape[0]
    skel_width = pivot_b.shape[0]
    points = jnp.arange(points_count, dtype=jnp.int32)
    living = jnp.arange(skel_width, dtype=jnp.int32) < rank_b
    select = ((pivot_b[:, None] == points[None, :]) & living[:, None]).astype(jnp.bfloat16)
    redundant = 1.0 - jnp.sum(select.astype(jnp.float32), axis=0)
    coefficients = jnp.where(
        living[:, None] & (redundant[None, :] > 0.5), interp_b, jnp.zeros_like(interp_b)
    )
    placed = jnp.einsum("kp,kq->pq", coefficients, select, preferred_element_type=jnp.float32)
    compress = (redundant[:, None] * (jnp.eye(points_count, dtype=jnp.float32) - placed)).astype(
        jnp.bfloat16
    )
    halfway = jnp.dot(redinv_b, compress, preferred_element_type=jnp.float32).astype(jnp.bfloat16)
    eliminator = jnp.einsum(
        "pq,pr->qr", compress, halfway, preferred_element_type=jnp.float32
    ).astype(jnp.bfloat16)
    lifted = jnp.einsum(
        "nkp,pq->nkq", back_b, eliminator, preferred_element_type=jnp.float32
    ).astype(jnp.bfloat16)
    return -jnp.einsum("nkq,nql->nkl", lifted, near_b, preferred_element_type=jnp.float32)


def body(self_blk, near, back, interp, redinv, ranks, pivots, neighbors, parent):
    gx_count = lax.axis_size("gx")
    lane_count = lax.axis_size("gy")
    box_dev = self_blk.shape[0]
    skel_width = self_blk.shape[1]
    block_size = skel_width * skel_width
    updates = jax.vmap(box_terms)(near, back, interp, redinv, ranks, pivots)
    entry_count = box_dev * neighbors.shape[1]
    flattened = updates.reshape(entry_count, block_size)
    targets = neighbors.reshape(entry_count)
    dest_row = targets // box_dev // lane_count
    dest_slot = targets % box_dev
    spread = (
        (dest_row * box_dev + dest_slot)[:, None]
        == jnp.arange(gx_count * box_dev, dtype=jnp.int32)[None, :]
    ).astype(jnp.float32)
    outgoing = jnp.einsum("us,uk->sk", spread, flattened, precision=lax.Precision.HIGHEST).astype(
        jnp.bfloat16
    )
    incoming = lax.all_to_all(
        outgoing.reshape(gx_count, box_dev, block_size),
        "gx",
        split_axis=0,
        concat_axis=0,
        tiled=True,
    )
    summed = jnp.sum(incoming, axis=0, dtype=jnp.float32)
    living = jnp.arange(skel_width, dtype=jnp.int32)[None, :] < ranks[:, None]
    masking = living[:, :, None] & living[:, None, :]
    merged = jnp.where(masking, self_blk + summed.reshape(box_dev, skel_width, skel_width), 0.0)
    row_boxes = lane_count * box_dev
    row_start = lax.axis_index("gx") * row_boxes
    local_slot = parent - row_start
    placement = (local_slot[:, None] == jnp.arange(row_boxes, dtype=jnp.int32)[None, :]).astype(
        jnp.float32
    )
    spread_out = jnp.einsum(
        "bq,bk->qk", placement, merged.reshape(box_dev, block_size), precision=lax.Precision.HIGHEST
    )
    result = lax.psum_scatter(spread_out, "gy", scatter_dimension=0, tiled=True)
    return result.reshape(box_dev, skel_width, skel_width)


def solution(mesh):
    placed = (
        P(("gx", "gy"), None, None),
        P(("gx", "gy"), None, None, None),
        P(("gx", "gy"), None, None, None),
        P(("gx", "gy"), None, None),
        P(("gx", "gy"), None, None),
        P(("gx", "gy")),
        P(("gx", "gy"), None),
        P(("gx", "gy"), None),
        P(("gx", "gy")),
    )
    return jax.shard_map(
        body, mesh=mesh, in_specs=placed, out_specs=P(("gx", "gy"), None, None), check_vma=False
    )
```

profile of v0, /device:TPU:0, one launch (start us, length us, event | category | flops | bytes accessed | tf_op | source)
XLA Modules:
  0.0 89.5 jit_solution(7814409902789188969)
XLA Ops:
  6.5 0.8 iota_compare_fusion.4
  7.4 0.8 convert_reduce_fusion.1
  8.2 0.1 fusion.9
  8.3 1.7 %multiply_convert_fusion = bf16[2,512,512]{2,1,0:T(8,128)(2,1)S(1)} fusion(f32[512,512]{1,0:T(8,128)S(1)} %fusion.9, f32[2,512]{1,0:T(2,128)S(1)} %broadcast_subtract_fusion, bf16[2,128,512]{2,1,0:T(8,128)(2,1)} %param.12, s32[2,128]{1,0:T(2,128)} %param.15, pred[2,512]{1,0:T(4,128)(4,1)S(1)} %broadcast_compare_fusion, pred[2,128]{1,0:T(4,128)(4,1)S(1)} %iota_compare_fusion.4), kind=kOutput, calls=%fused_computation.4 | convolution fusion | flops 136314880 | bytes 2365696 | tf_op jit(solution)/shard_map/vmap(kp,kq->pq)/dot_general | solution.py:17
  10.0 2.5 %fusion.8 = bf16[2,512,512,1]{2,1,3,0:T(8,128)(2,1)} fusion(bf16[2,512,512]{2,1,0:T(8,128)(2,1)S(1)} %multiply_convert_fusion, bf16[2,512,512]{2,1,0:T(8,128)(2,1)S(1)} %copy-done), kind=kOutput, calls=%fused_computation.9 | convolution fusion | flops 1074790400 | bytes 3145728 | tf_op jit(solution)/shard_map/vmap(pq,pr->qr)/dot_general | solution.py:22
  12.5 6.5 %fusion.5 = f32[2,14,128,128]{3,2,1,0:T(8,128)S(1)} fusion(bf16[2,14,512,128]{3,2,1,0:T(8,128)(2,1)} %param.10, bf16[2,512,512,1]{2,1,3,0:T(8,128)(2,1)} %fusion.8, bf16[2,14,128,512]{3,2,1,0:T(8,128)(2,1)} %param.11), kind=kOutput, calls=%fused_computation.6 | convolution fusion | flops 2351104000 | bytes 10223616 | tf_op jit(solution)/shard_map/vmap(nkq,nql->nkl)/dot_general | solution.py:28
  19.0 0.2 pad
  19.3 0.0 copy-start.2
  19.3 1.2 %copy.14 = f32[4,8,128,128]{3,1,2,0:T(8,128)S(1)} copy(f32[4,8,128,128]{3,2,1,0:T(8,128)S(1)} %bitcast.39) | data formatting | bytes 4194304
  20.5 0.1 reshape.137
  20.6 0.0 copy-start.3
  20.6 1.7 %convolution_convert_fusion = bf16[16,16384]{1,0:T(8,128)(2,1)} fusion(f32[28,16384]{1,0:T(8,128)S(1)} %bitcast.38, s32[28]{0:T(128)S(1)} %fusion.25), kind=kOutput, calls=%fused_computation | convolution fusion | flops 88342976 | bytes 2359408 | tf_op jit(solution)/shard_map/us,uk->sk/dot_general | solution.py:47
  22.3 2.2 %reshape.139 = bf16[8,2,16384]{2,1,0:T(2,128)(2,1)} reshape(bf16[16,16384]{1,0:T(8,128)(2,1)} %convolution_convert_fusion) | data formatting | bytes 1048576 | tf_op jit(solution)/shard_map/reshape | solution.py:51
  24.5 7.3 %all-to-all-start = ((bf16[8,2,16384]{2,1,0:T(2,128)(2,1)}), bf16[8,2,16384]{2,1,0:T(2,128)(2,1)S(1)}, u32[]{:S(2)}, u32[]{:S(2)}) async-start(bf16[8,2,16384]{2,1,0:T(2,128)(2,1)} %reshape.139), calls=%async_computation | async-start | bytes 1048576 | tf_op jit(solution)/shard_map/all_to_all | solution.py:50
  31.8 0.0 all-reduce.3.cloned.1.call-start
  31.9 14.4 %all-to-all-done = bf16[8,2,16384]{2,1,0:T(2,128)(2,1)S(1)} async-done(((bf16[8,2,16384]{2,1,0:T(2,128)(2,1)}), bf16[8,2,16384]{2,1,0:T(2,128)(2,1)S(1)}, u32[]{:S(2)}, u32[]{:S(2)}) %all-to-all-start) | async-done | bytes 524320 | tf_op jit(solution)/shard_map/all_to_all | solution.py:50
  46.3 0.5 convert_reduce_fusion
  46.8 0.1 fusion.20
  46.9 1.3 %fusion.16 = f32[8,16384]{1,0:T(8,128)} fusion(f32[1,2,128,128]{3,2,1,0:T(8,128)S(1)} %fusion.20, s32[2]{0:T(128)S(1)} %broadcast_subtract_fusion.1), kind=kOutput, calls=%fused_computation.22 | convolution fusion | flops 3145744 | bytes 655368 | tf_op jit(solution)/shard_map/bq,bk->qk/dot_general | solution.py:67
  48.2 0.0 all-reduce.3.cloned.1.call-update
  48.2 0.6 dynamic-slice
  49.5 31.4 %all-reduce.3.cloned.1.call-done = f32[8,16384]{1,0:T(8,128)} async-done(((f32[8,16384]{1,0:T(8,128)}), f32[8,16384]{1,0:T(8,128)}) %all-reduce.3.cloned.1.call-update) | async-done | bytes 524304
  80.9 1.1 %dynamic-slice_bitcast_fusion = f32[1,2,128,128]{3,1,2,0:T(2,128)S(1)} fusion(f32[8,16384]{1,0:T(8,128)} %all-reduce.3.cloned.1.call-done, u32[]{:T(128)S(6)} %multiply.1), kind=kLoop, calls=%fused_computation.28 | loop fusion | bytes 262148
  82.0 0.7 copy.24
  (12 shorter events, 0.1 us)
Async XLA Ops:
  6.5 3.5 %copy-start = (bf16[2,512,512]{2,1,0:T(8,128)(2,1)S(1)}, bf16[2,512,512]{2,1,0:T(8,128)(2,1)}, u32[]{:S(2)}) copy-start(bf16[2,512,512]{2,1,0:T(8,128)(2,1)} %param.13) | copy-start | bytes 3145732
  19.3 1.2 %copy-start.2 = (s32[2,14]{1,0:T(2,128)S(1)}, s32[2,14]{1,0:T(2,128)}, u32[]{:S(2)}) copy-start(s32[2,14]{1,0:T(2,128)} %param.16) | copy-start | bytes 340
  20.6 11.2 %copy-start.3 = (s32[2]{0:T(128)S(1)}, s32[2]{0:T(128)}, u32[]{:S(2)}) copy-start(s32[2]{0:T(128)} %param.17) | copy-start | bytes 28
  20.6 26.1 %copy-start.1 = (f32[2,128,128]{2,1,0:T(8,128)S(1)}, f32[2,128,128]{2,1,0:T(8,128)}, u32[]{:S(2)}) copy-start(f32[2,128,128]{2,1,0:T(8,128)} %param.9) | copy-start | bytes 393220
  22.3 25.9 %copy-start.4 = (u32[32]{0:T(128)S(1)}, u32[32]{0:T(128)}, u32[]{:S(2)}) copy-start(u32[32]{0:T(128)} %constant.64) | copy-start | bytes 388
  24.5 21.8 %all-to-all-start = ((bf16[8,2,16384]{2,1,0:T(2,128)(2,1)}), bf16[8,2,16384]{2,1,0:T(2,128)(2,1)S(1)}, u32[]{:S(2)}, u32[]{:S(2)}) async-start(bf16[8,2,16384]{2,1,0:T(2,128)(2,1)} %reshape.139), calls=%async_computation | async-start | bytes 1048576 | tf_op jit(solution)/shard_map/all_to_all | solution.py:50
  31.8 49.1 %all-reduce.3.cloned.1.call-start = ((), (), s32[]{:S(2)}) async-start(), calls=%async_computation.1 | async-start | bytes 1048576
Sparse Core Ops, SparseCore 0:
  48.3 32.4 all-reduce.2
where the time goes:
time: 89.8 us; the launch traced here: 89.5 us
  waiting for transfers between devices  45.8 us (51%)
  between operations  14.2 us (16%)
  matrix products  13.7 us (15%)
  starting transfers between devices  7.32 us (8%)
  local copies, waits for them, and re-layouts  6.06 us (7%)
  other arithmetic  2.38 us (3%)
    unnamed x2, waiting for transfers between devices  31.4 us
    all_to_all x1, waiting for transfers between devices, body(): lax.all_to_all(outgoing.reshape(gx_count, box_dev, block_size), 'gx', spl...  14.4 us
    all_to_all x1, starting transfers between devices, body(): lax.all_to_all(outgoing.reshape(gx_count, box_dev, block_size), 'gx', spl...  7.28 us
    dot_general x1, matrix products, box_terms(): jnp.einsum('nkq,nql->nkl', lifted, near_b, preferred_element_type=jnp.flo...  6.5 us
    unnamed x15, local copies, waits for them, and re-layouts  3.8 us
    dot_general x1, matrix products, box_terms(): jnp.einsum('pq,pr->qr', compress, halfway, preferred_element_type=jnp.flo...  2.49 us
    reshape x1, local copies, waits for them, and re-layouts, body(): outgoing.reshape(gx_count, box_dev, block_size)  2.18 us
  transfers between devices with their start and end apart: 2, of which 2 were waited for; matrix products, arithmetic and copies ran while one was open for 1% of the time, Pallas kernels for 0%

commit v1 on v0

v1 whole, which is shorter than its diff:
```python
import jax
import jax.numpy as jnp
from jax import lax
from jax.experimental import pallas as pl
from jax.experimental.pallas import tpu as pltpu
from jax.sharding import PartitionSpec as P

GX = "gx"
GY = "gy"


def nt(a, b):
    return lax.dot_general(a, b, (((1,), (1,)), ((), ())), preferred_element_type=jnp.float32)


def nn(a, b):
    return jnp.dot(a, b, preferred_element_type=jnp.float32)


def eliminator_of(interp, redinv, pivot_row, rank):
    width, points = interp.shape
    point_col = lax.broadcasted_iota(jnp.int32, (points, width), 0)
    skel_row = lax.broadcasted_iota(jnp.int32, (points, width), 1)
    hit = (point_col == pivot_row) & (skel_row < rank)
    select_t = jnp.where(hit, 1.0, 0.0).astype(jnp.bfloat16)
    ones = jnp.ones((8, width), jnp.bfloat16)
    chosen_row = nt(ones, select_t)[:1]
    redundant_row = chosen_row < 0.5
    redundant_col = jnp.max(jnp.where(hit, 1.0, 0.0), axis=1, keepdims=True) < 0.5
    living = lax.broadcasted_iota(jnp.int32, (width, points), 0) < rank
    coefficients = jnp.where(living & redundant_row, interp, jnp.zeros_like(interp))
    half_skel = (-nt(redinv, coefficients)).astype(jnp.bfloat16)
    halfway = jnp.where(redundant_row, redinv, nt(half_skel, select_t).astype(jnp.bfloat16))
    elim_skel = (-nn(coefficients, halfway)).astype(jnp.bfloat16)
    return jnp.where(redundant_col, halfway, nn(select_t, elim_skel).astype(jnp.bfloat16))


def make_kernel(box_dev, near_count, gx_count, lane_count, width, points, parts):
    def kernel(ranks, neighbors, pivots, interp_hbm, redinv_hbm, back_hbm, near_hbm, *rest):
        outs = rest[:gx_count]
        interp_v, redinv_v, back_v, near_v, lifted_v, table, sems = rest[gx_count:]
        per = near_count // parts
        small, bulk = [], []
        for b in range(box_dev):
            small.append(
                (
                    pltpu.make_async_copy(interp_hbm.at[b], interp_v.at[b], sems.at[b, 0]),
                    pltpu.make_async_copy(redinv_hbm.at[b], redinv_v.at[b], sems.at[b, 1]),
                )
            )
        for b in range(box_dev):
            copies = []
            for c in range(parts):
                part = pl.ds(c * per, per)
                copies.append(
                    pltpu.make_async_copy(
                        back_hbm.at[b, part], back_v.at[b, part], sems.at[b, 3 + c]
                    )
                )
            bulk.append(copies)
        near_copies = [
            pltpu.make_async_copy(near_hbm.at[b], near_v.at[b], sems.at[b, 2])
            for b in range(box_dev)
        ]
        for pair in small:
            pair[0].start()
            pair[1].start()
        for copies in bulk:
            for copy in copies:
                copy.start()
        for copy in near_copies:
            copy.start()
        me = lax.axis_index(GX)
        for b in range(box_dev):
            for u in range(gx_count * box_dev):
                table[b, u] = near_count
        for b in range(box_dev):
            for n in range(near_count):
                target = neighbors[b, n]
                row = target // (box_dev * lane_count)
                table[b, (row ^ me) * box_dev + target % box_dev] = n
            lifted_v[b, near_count] = jnp.zeros((width, points), jnp.bfloat16)
        elims = []
        for b in range(box_dev):
            small[b][0].wait()
            small[b][1].wait()
            elims.append(
                eliminator_of(interp_v[b], redinv_v[b], pivots[pl.ds(b, 1), :], ranks[b])
            )
        for b in range(box_dev):
            for c in range(parts):
                bulk[b][c].wait()
                rows = back_v[b, pl.ds(c * per, per)].reshape(per * width, points)
                lifted_v[b, pl.ds(c * per, per)] = (
                    nn(rows, elims[b]).astype(jnp.bfloat16).reshape(per, width, points)
                )
        for copy in near_copies:
            copy.wait()
        for k in range(gx_count):
            for s in range(box_dev):
                total = None
                for b in range(box_dev):
                    n = table[b, k * box_dev + s]
                    term = nn(lifted_v[b, n], near_v[b, jnp.minimum(n, near_count - 1)])
                    total = term if total is None else total + term
                outs[k][s] = (-total).astype(jnp.bfloat16)

    return kernel


def local_updates(near, back, interp, redinv, ranks, pivots, neighbors):
    box_dev, near_count, points, width = near.shape
    gx_count = lax.axis_size(GX)
    lane_count = lax.axis_size(GY)
    parts = 2 if near_count % 2 == 0 else 1
    kernel = make_kernel(box_dev, near_count, gx_count, lane_count, width, points, parts)
    smem = pl.BlockSpec(memory_space=pltpu.SMEM)
    vmem = pl.BlockSpec(memory_space=pltpu.VMEM)
    anywhere = pl.BlockSpec(memory_space=pl.ANY)
    bf16 = jnp.bfloat16
    return pl.pallas_call(
        kernel,
        out_shape=[jax.ShapeDtypeStruct((box_dev, width, width), bf16)] * gx_count,
        in_specs=[smem, smem, vmem, anywhere, anywhere, anywhere, anywhere],
        out_specs=[vmem] * gx_count,
        scratch_shapes=[
            pltpu.VMEM((box_dev, width, points), bf16),
            pltpu.VMEM((box_dev, points, points), bf16),
            pltpu.VMEM((box_dev, near_count, width, points), bf16),
            pltpu.VMEM((box_dev, near_count, points, width), bf16),
            pltpu.VMEM((box_dev, near_count + 1, width, points), bf16),
            pltpu.SMEM((box_dev, gx_count * box_dev), jnp.int32),
            pltpu.SemaphoreType.DMA((box_dev, 3 + parts)),
        ],
        compiler_params=pltpu.CompilerParams(vmem_limit_bytes=40 * 1024 * 1024),
        name="updates",
    )(ranks, neighbors, pivots, interp, redinv, back, near)


def swap(value, axis, size, k):
    return lax.ppermute(value, axis, [(a, a ^ k) for a in range(size)])


def body(self_blk, near, back, interp, redinv, ranks, pivots, neighbors, parent):
    gx_count = lax.axis_size(GX)
    lane_count = lax.axis_size(GY)
    box_dev, width = self_blk.shape[:2]
    parts = local_updates(near, back, interp, redinv, ranks, pivots, neighbors)
    arrived = [parts[0]]
    for k in range(1, gx_count):
        arrived.append(swap(parts[k], GX, gx_count, k))
    summed = sum(a.astype(jnp.float32) for a in arrived)
    living = jnp.arange(width, dtype=jnp.int32)[None, :] < ranks[:, None]
    masking = living[:, :, None] & living[:, None, :]
    merged = jnp.where(masking, self_blk + summed, 0.0)
    row = parent - lax.axis_index(GX) * (lane_count * box_dev)
    lane = lax.axis_index(GY)
    result = None
    for k in range(lane_count):
        slots = []
        for s in range(box_dev):
            here = row == (lane ^ k) * box_dev + s
            slots.append(jnp.sum(jnp.where(here[:, None, None], merged, 0.0), axis=0))
        placed = jnp.stack(slots)
        if k:
            placed = swap(placed.astype(jnp.bfloat16), GY, lane_count, k).astype(jnp.float32)
        result = placed if result is None else result + placed
    return result


def solution(mesh):
    split = (GX, GY)
    placed = (
        P(split, None, None),
        P(split, None, None, None),
        P(split, None, None, None),
        P(split, None, None),
        P(split, None, None),
        P(split),
        P(split, None),
        P(split, None),
        P(split),
    )
    return jax.shard_map(
        body, mesh=mesh, in_specs=placed, out_specs=P(split, None, None), check_vma=False
    )
```

time: 89.8 us -> 43.6 us (0.49)
  waiting for transfers between devices: 45.8 us -> 10.3 us
  between operations: 14.2 us -> 0.07 us
  matrix products: 13.7 us -> 0 us
  Pallas kernels: 0 us -> 8.76 us
  starting transfers between devices: 7.32 us -> 14.9 us
  local copies, waits for them, and re-layouts: 6.06 us -> 8.27 us
  other arithmetic: 2.38 us -> 0.97 us
    unnamed x2 -> x0, waiting for transfers between devices: 31.4 us -> none
    ppermute x0 -> x10, starting transfers between devices: none -> 14.9 us  [swap(): return lax.ppermute(value, axis, [(a, a ^ k) for a in range(size)])]
    all_to_all x1 -> x0, waiting for transfers between devices: 14.4 us -> none  [body(): lax.all_to_all(outgoing.reshape(gx_count, box_dev, block_size), 'gx', spl...]
    dot_general x5 -> x0, matrix products: 13.7 us -> none  [the longest x1 6.5 us: box_terms(): jnp.einsum('nkq,nql->nkl', lifted, near_b, preferred_element_type=jnp.flo...]
    ppermute x0 -> x10, waiting for transfers between devices: none -> 10.3 us  [swap(): return lax.ppermute(value, axis, [(a, a ^ k) for a in range(size)])]
    pallas_call x0 -> x1, Pallas kernels: none -> 8.76 us  [local_updates(): pl.pallas_call(kernel, out_shape=[jax.ShapeDtypeStruct((box_dev, width, w...]
    all_to_all x1 -> x0, starting transfers between devices: 7.28 us -> none  [body(): lax.all_to_all(outgoing.reshape(gx_count, box_dev, block_size), 'gx', spl...]
    unnamed x15 -> x20, local copies, waits for them, and re-layouts: 3.8 us -> 8.27 us
  transfers between devices with their start and end apart: 2 -> 10, of which waited for: 2 -> 4; matrix products, arithmetic and copies ran while one was open for 1% -> 0% of each run, Pallas kernels for 0% -> 0%
where the time goes in v1:
time: 43.6 us; the launch traced here: 43.3 us
  starting transfers between devices  14.9 us (34%)
  waiting for transfers between devices  10.3 us (24%)
  Pallas kernels  8.76 us (20%)
  local copies, waits for them, and re-layouts  8.27 us (19%)
  other arithmetic  0.97 us (2%)
    ppermute x10, starting transfers between devices, swap(): return lax.ppermute(value, axis, [(a, a ^ k) for a in range(size)])  14.9 us
    ppermute x10, waiting for transfers between devices, swap(): return lax.ppermute(value, axis, [(a, a ^ k) for a in range(size)])  10.3 us
    pallas_call x1, Pallas kernels, local_updates(): pl.pallas_call(kernel, out_shape=[jax.ShapeDtypeStruct((box_dev, width, w...  8.76 us
    unnamed x20, local copies, waits for them, and re-layouts  8.27 us
  transfers between devices with their start and end apart: 10, of which 4 were waited for; matrix products, arithmetic and copies ran while one was open for 0% of the time, Pallas kernels for 0%

profile of v1, /device:TPU:0, one launch (start us, length us, event | category | flops | bytes accessed | tf_op | source)
XLA Modules:
  0.0 43.3 jit_solution(11745818205572863746)
XLA Ops:
  0.0 2.0 %copy-done = bf16[2,14,128,512]{3,2,1,0:T(8,128)(2,1)S(1)} copy-done((bf16[2,14,128,512]{3,2,1,0:T(8,128)(2,1)S(1)}, bf16[2,14,128,512]{3,2,1,0:T(8,128)(2,1)}, u32[]{:S(2)}) %copy-start) | copy-done | bytes 3670040
  2.0 2.0 %copy-done.1 = bf16[2,14,512,128]{3,2,1,0:T(8,128)(2,1)S(1)} copy-done((bf16[2,14,512,128]{3,2,1,0:T(8,128)(2,1)S(1)}, bf16[2,14,512,128]{3,2,1,0:T(8,128)(2,1)}, u32[]{:S(2)}) %copy-start.1) | copy-done | bytes 3670040
  4.1 1.2 %copy-done.2 = bf16[2,512,512]{2,1,0:T(8,128)(2,1)S(1)} copy-done((bf16[2,512,512]{2,1,0:T(8,128)(2,1)S(1)}, bf16[2,512,512]{2,1,0:T(8,128)(2,1)}, u32[]{:S(2)}) %copy-start.2) | copy-done | bytes 1048600
  5.3 0.9 %copy-done.3 = bf16[2,128,512]{2,1,0:T(8,128)(2,1)S(1)} copy-done((bf16[2,128,512]{2,1,0:T(8,128)(2,1)S(1)}, bf16[2,128,512]{2,1,0:T(8,128)(2,1)}, u32[]{:S(2)}) %copy-start.3) | copy-done | bytes 262168
  6.3 0.7 %copy-done.4 = s32[2,14]{1,0:T(2,128)S(1)} copy-done((s32[2,14]{1,0:T(2,128)S(1)}, s32[2,14]{1,0:T(2,128)}, u32[]{:S(2)}) %copy-start.4) | copy-done | bytes 136
  6.9 0.7 %copy-done.5 = s32[2,128]{1,0:T(2,128)S(1)} copy-done((s32[2,128]{1,0:T(2,128)S(1)}, s32[2,128]{1,0:T(2,128)}, u32[]{:S(2)}) %copy-start.5) | copy-done | bytes 1048
  7.6 0.7 %copy-done.6 = s32[2]{0:T(128)S(1)} copy-done((s32[2]{0:T(128)S(1)}, s32[2]{0:T(128)}, u32[]{:S(2)}) %copy-start.6) | copy-done | bytes 32
  8.3 8.8 %updates.1 = (bf16[2,128,128]{2,1,0:T(8,128)(2,1)S(1)}, bf16[2,128,128]{2,1,0:T(8,128)(2,1)S(1)}, bf16[2,128,128]{2,1,0:T(8,128)(2,1)S(1)}, bf16[2,128,128]{2,1,...) custom-call(s32[2]{0:T(128)S(1)} %copy-done.6, ...), custom_call_target="tpu_custom_call" | custom-call | tf_op jit(solution)/shard_map/updates/pallas_call | solution.py:121
  17.0 3.0 %collective-permute-start = (bf16[2,128,128]{2,1,0:T(8,128)(2,1)S(1)}, bf16[2,128,128]{2,1,0:T(8,128)(2,1)S(1)}, u32[]{:S(2)}, u32[]{:S(2)}) collective-permute-start(bf16[2,128,128]{2,1,0:T(8,128)(2,1)S(1)} %get-tuple-element.14), channel_id=1, source_target_pairs={{0,4},{4,0},{8,12},{12,8},{16,20},{20,16},{24,28},{28,24},{1,5},{5... | collective-permute-start | bytes 196616 | tf_op jit(solution)/shard_map/ppermute | solution.py:141
  20.1 1.6 %collective-permute-start.1 = (bf16[2,128,128]{2,1,0:T(8,128)(2,1)S(1)}, bf16[2,128,128]{2,1,0:T(8,128)(2,1)S(1)}, u32[]{:S(2)}, u32[]{:S(2)}) collective-permute-start(bf16[2,128,128]{2,1,0:T(8,128)(2,1)S(1)} %get-tuple-element.15), channel_id=1, source_target_pairs={{0,8},{4,12},{8,0},{12,4},{16,24},{20,28},{24,16},{28,20},{1,9},{5... | collective-permute-start | bytes 196616 | tf_op jit(solution)/shard_map/ppermute | solution.py:141
  21.7 3.0 %collective-permute-start.3 = (bf16[2,128,128]{2,1,0:T(8,128)(2,1)S(1)}, bf16[2,128,128]{2,1,0:T(8,128)(2,1)S(1)}, u32[]{:S(2)}, u32[]{:S(2)}) collective-permute-start(bf16[2,128,128]{2,1,0:T(8,128)(2,1)S(1)} %get-tuple-element.17), channel_id=1, source_target_pairs={{0,16},{4,20},{8,24},{12,28},{16,0},{20,4},{24,8},{28,12},{1,17},{... | collective-permute-start | bytes 196616 | tf_op jit(solution)/shard_map/ppermute | solution.py:141
  24.7 1.3 %collective-permute-start.4 = (bf16[2,128,128]{2,1,0:T(8,128)(2,1)S(1)}, bf16[2,128,128]{2,1,0:T(8,128)(2,1)S(1)}, u32[]{:S(2)}, u32[]{:S(2)}) collective-permute-start(bf16[2,128,128]{2,1,0:T(8,128)(2,1)S(1)} %get-tuple-element.18), channel_id=1, source_target_pairs={{0,20},{4,16},{8,28},{12,24},{16,4},{20,0},{24,12},{28,8},{1,21},{... | collective-permute-start | bytes 196616 | tf_op jit(solution)/shard_map/ppermute | solution.py:141
  26.0 3.7 %collective-permute-start.5 = (bf16[2,128,128]{2,1,0:T(8,128)(2,1)S(1)}, bf16[2,128,128]{2,1,0:T(8,128)(2,1)S(1)}, u32[]{:S(2)}, u32[]{:S(2)}) collective-permute-start(bf16[2,128,128]{2,1,0:T(8,128)(2,1)S(1)} %get-tuple-element.19), channel_id=1, source_target_pairs={{0,24},{4,28},{8,16},{12,20},{16,8},{20,12},{24,0},{28,4},{1,25},{... | collective-permute-start | bytes 196616 | tf_op jit(solution)/shard_map/ppermute | solution.py:141
  29.6 0.1 collective-permute-start.6
  29.7 0.1 iota_compare_fusion
  29.8 5.1 %collective-permute-done.4 = bf16[2,128,128]{2,1,0:T(8,128)(2,1)S(1)} collective-permute-done((bf16[2,128,128]{2,1,0:T(8,128)(2,1)S(1)}, bf16[2,128,128]{2,1,0:T(8,128)(2,1)S(1)}, u32[]{:S(2)}, u32[]{:S(2)}) %collective-permute-start.4) | collective-permute-done | bytes 65568 | tf_op jit(solution)/shard_map/ppermute | solution.py:141
  34.8 1.9 %collective-permute-done.6 = bf16[2,128,128]{2,1,0:T(8,128)(2,1)S(1)} collective-permute-done((bf16[2,128,128]{2,1,0:T(8,128)(2,1)S(1)}, bf16[2,128,128]{2,1,0:T(8,128)(2,1)S(1)}, u32[]{:S(2)}, u32[]{:S(2)}) %collective-permute-start.6) | collective-permute-done | bytes 65568 | tf_op jit(solution)/shard_map/ppermute | solution.py:141
  36.7 0.2 select_reduce_fusion.5
  36.9 1.6 %collective-permute-start.8 = (bf16[2,128,128]{2,1,0:T(8,128)(2,1)S(1)}, bf16[2,128,128]{2,1,0:T(8,128)(2,1)S(1)}, u32[]{:S(2)}, u32[]{:S(2)}) collective-permute-start(bf16[2,128,128]{2,1,0:T(8,128)(2,1)S(1)} %pad_maximum_fusion.1), channel_id=1, source_target_pairs={{0,2},{1,3},{2,0},{3,1},{4,6},{5,7},{6,4},{7,5},{8,10},{9,11},{10,... | collective-permute-start | bytes 196616 | tf_op jit(solution)/shard_map/ppermute | solution.py:141
  38.5 0.1 collective-permute-start.9
  38.6 0.7 %collective-permute-start.7 = (bf16[2,128,128]{2,1,0:T(8,128)(2,1)S(1)}, bf16[2,128,128]{2,1,0:T(8,128)(2,1)S(1)}, u32[]{:S(2)}, u32[]{:S(2)}) collective-permute-start(bf16[2,128,128]{2,1,0:T(8,128)(2,1)S(1)} %pad_maximum_fusion), channel_id=1, source_target_pairs={{0,1},{1,0},{2,3},{3,2},{4,5},{5,4},{6,7},{7,6},{8,9},{9,8},{10,11... | collective-permute-start | bytes 196616 | tf_op jit(solution)/shard_map/ppermute | solution.py:141
  39.2 2.0 %collective-permute-done.8 = bf16[2,128,128]{2,1,0:T(8,128)(2,1)S(1)} collective-permute-done((bf16[2,128,128]{2,1,0:T(8,128)(2,1)S(1)}, bf16[2,128,128]{2,1,0:T(8,128)(2,1)S(1)}, u32[]{:S(2)}, u32[]{:S(2)}) %collective-permute-start.8) | collective-permute-done | bytes 65568 | tf_op jit(solution)/shard_map/ppermute | solution.py:141
  41.2 1.4 %collective-permute-done.9 = bf16[2,128,128]{2,1,0:T(8,128)(2,1)S(1)} collective-permute-done((bf16[2,128,128]{2,1,0:T(8,128)(2,1)S(1)}, bf16[2,128,128]{2,1,0:T(8,128)(2,1)S(1)}, u32[]{:S(2)}, u32[]{:S(2)}) %collective-permute-start.9) | collective-permute-done | bytes 65568 | tf_op jit(solution)/shard_map/ppermute | solution.py:141
  42.6 0.7 %fusion.1 = f32[2,128,128]{2,1,0:T(8,128)} fusion(f32[1,128,128]{2,1,0:T(8,128)S(1)} %bitcast.20, f32[1,128,128]{2,1,0:T(8,128)S(1)} %bitcast.21, bf16[2,128,128]{2,1,0:T(8,128)(2,1)S(1)} %collective-permute-done.9, bf16[2,128,128]{2,1,0:T(8,128)(2,1)S(1)} %collective-permute-done.8, bf16[2,128,128]{2,1,0:T(8,128)(2,1)S(1)} %collective-permute-done.7), kind=kLoop, calls=%fused_computation.2 | loop fusion | flops 229376 | bytes 458752 | tf_op jit(solution)/shard_map/add | solution.py:167
  (25 shorter events, 0.1 us)
Async XLA Ops:
  0.0 2.0 %copy-start = (bf16[2,14,128,512]{3,2,1,0:T(8,128)(2,1)S(1)}, bf16[2,14,128,512]{3,2,1,0:T(8,128)(2,1)}, u32[]{:S(2)}) copy-start(bf16[2,14,128,512]{3,2,1,0:T(8,128)(2,1)} %back_hbm.1) | copy-start | bytes 11010052
  2.0 2.0 %copy-start.1 = (bf16[2,14,512,128]{3,2,1,0:T(8,128)(2,1)S(1)}, bf16[2,14,512,128]{3,2,1,0:T(8,128)(2,1)}, u32[]{:S(2)}) copy-start(bf16[2,14,512,128]{3,2,1,0:T(8,128)(2,1)} %near_hbm.1) | copy-start | bytes 11010052
  4.1 1.2 %copy-start.2 = (bf16[2,512,512]{2,1,0:T(8,128)(2,1)S(1)}, bf16[2,512,512]{2,1,0:T(8,128)(2,1)}, u32[]{:S(2)}) copy-start(bf16[2,512,512]{2,1,0:T(8,128)(2,1)} %redinv_hbm.1) | copy-start | bytes 3145732
  5.3 0.9 %copy-start.3 = (bf16[2,128,512]{2,1,0:T(8,128)(2,1)S(1)}, bf16[2,128,512]{2,1,0:T(8,128)(2,1)}, u32[]{:S(2)}) copy-start(bf16[2,128,512]{2,1,0:T(8,128)(2,1)} %interp_hbm.1) | copy-start | bytes 786436
  6.3 0.7 %copy-start.4 = (s32[2,14]{1,0:T(2,128)S(1)}, s32[2,14]{1,0:T(2,128)}, u32[]{:S(2)}) copy-start(s32[2,14]{1,0:T(2,128)} %neighbors.1) | copy-start | bytes 340
  6.9 0.7 %copy-start.5 = (s32[2,128]{1,0:T(2,128)S(1)}, s32[2,128]{1,0:T(2,128)}, u32[]{:S(2)}) copy-start(s32[2,128]{1,0:T(2,128)} %pivots.1) | copy-start | bytes 3076
  7.6 0.7 %copy-start.6 = (s32[2]{0:T(128)S(1)}, s32[2]{0:T(128)}, u32[]{:S(2)}) copy-start(s32[2]{0:T(128)} %ranks.1) | copy-start | bytes 28
  8.3 17.7 %copy-start.9 = (s32[2]{0:T(128)S(1)}, s32[2]{0:T(128)}, u32[]{:S(2)}) copy-start(s32[2]{0:T(128)} %param.17) | copy-start | bytes 28
  8.3 21.4 %copy-start.7 = (s32[2]{0:T(128)S(1)}, s32[2]{0:T(128)}, u32[]{:S(2)}) copy-start(s32[2]{0:T(128)} %ranks.1) | copy-start | bytes 28
  8.3 28.4 %copy-start.8 = (f32[2,128,128]{2,1,0:T(8,128)S(1)}, f32[2,128,128]{2,1,0:T(8,128)}, u32[]{:S(2)}) copy-start(f32[2,128,128]{2,1,0:T(8,128)} %param.9) | copy-start | bytes 393220
  17.0 8.9 %collective-permute-start = (bf16[2,128,128]{2,1,0:T(8,128)(2,1)S(1)}, bf16[2,128,128]{2,1,0:T(8,128)(2,1)S(1)}, u32[]{:S(2)}, u32[]{:S(2)}) collective-permute-start(bf16[2,128,128]{2,1,0:T(8,128)(2,1)S(1)} %get-tuple-element.14), channel_id=1, source_target_pairs={{0,4},{4,0},{8,12},{12,8},{16,20},{20,16},{24,28},{28,24},{1,5},{5... | collective-permute-start | bytes 196616 | tf_op jit(solution)/shard_map/ppermute | solution.py:141
  20.1 9.6 %collective-permute-start.1 = (bf16[2,128,128]{2,1,0:T(8,128)(2,1)S(1)}, bf16[2,128,128]{2,1,0:T(8,128)(2,1)S(1)}, u32[]{:S(2)}, u32[]{:S(2)}) collective-permute-start(bf16[2,128,128]{2,1,0:T(8,128)(2,1)S(1)} %get-tuple-element.15), channel_id=1, source_target_pairs={{0,8},{4,12},{8,0},{12,4},{16,24},{20,28},{24,16},{28,20},{1,9},{5... | collective-permute-start | bytes 196616 | tf_op jit(solution)/shard_map/ppermute | solution.py:141
  21.6 8.1 %collective-permute-start.2 = (bf16[2,128,128]{2,1,0:T(8,128)(2,1)S(1)}, bf16[2,128,128]{2,1,0:T(8,128)(2,1)S(1)}, u32[]{:S(2)}, u32[]{:S(2)}) collective-permute-start(bf16[2,128,128]{2,1,0:T(8,128)(2,1)S(1)} %get-tuple-element.16), channel_id=1, source_target_pairs={{0,12},{4,8},{8,4},{12,0},{16,28},{20,24},{24,20},{28,16},{1,13},{... | collective-permute-start | bytes 196616 | tf_op jit(solution)/shard_map/ppermute | solution.py:141
  21.7 8.1 %collective-permute-start.3 = (bf16[2,128,128]{2,1,0:T(8,128)(2,1)S(1)}, bf16[2,128,128]{2,1,0:T(8,128)(2,1)S(1)}, u32[]{:S(2)}, u32[]{:S(2)}) collective-permute-start(bf16[2,128,128]{2,1,0:T(8,128)(2,1)S(1)} %get-tuple-element.17), channel_id=1, source_target_pairs={{0,16},{4,20},{8,24},{12,28},{16,0},{20,4},{24,8},{28,12},{1,17},{... | collective-permute-start | bytes 196616 | tf_op jit(solution)/shard_map/ppermute | solution.py:141
  24.7 10.2 %collective-permute-start.4 = (bf16[2,128,128]{2,1,0:T(8,128)(2,1)S(1)}, bf16[2,128,128]{2,1,0:T(8,128)(2,1)S(1)}, u32[]{:S(2)}, u32[]{:S(2)}) collective-permute-start(bf16[2,128,128]{2,1,0:T(8,128)(2,1)S(1)} %get-tuple-element.18), channel_id=1, source_target_pairs={{0,20},{4,16},{8,28},{12,24},{16,4},{20,0},{24,12},{28,8},{1,21},{... | collective-permute-start | bytes 196616 | tf_op jit(solution)/shard_map/ppermute | solution.py:141
  26.0 8.9 %collective-permute-start.5 = (bf16[2,128,128]{2,1,0:T(8,128)(2,1)S(1)}, bf16[2,128,128]{2,1,0:T(8,128)(2,1)S(1)}, u32[]{:S(2)}, u32[]{:S(2)}) collective-permute-start(bf16[2,128,128]{2,1,0:T(8,128)(2,1)S(1)} %get-tuple-element.19), channel_id=1, source_target_pairs={{0,24},{4,28},{8,16},{12,20},{16,8},{20,12},{24,0},{28,4},{1,25},{... | collective-permute-start | bytes 196616 | tf_op jit(solution)/shard_map/ppermute | solution.py:141
  29.6 7.1 %collective-permute-start.6 = (bf16[2,128,128]{2,1,0:T(8,128)(2,1)S(1)}, bf16[2,128,128]{2,1,0:T(8,128)(2,1)S(1)}, u32[]{:S(2)}, u32[]{:S(2)}) collective-permute-start(bf16[2,128,128]{2,1,0:T(8,128)(2,1)S(1)} %get-tuple-element.20), channel_id=1, source_target_pairs={{0,28},{4,24},{8,20},{12,16},{16,12},{20,8},{24,4},{28,0},{1,29},{... | collective-permute-start | bytes 196616 | tf_op jit(solution)/shard_map/ppermute | solution.py:141
  36.9 4.3 %collective-permute-start.8 = (bf16[2,128,128]{2,1,0:T(8,128)(2,1)S(1)}, bf16[2,128,128]{2,1,0:T(8,128)(2,1)S(1)}, u32[]{:S(2)}, u32[]{:S(2)}) collective-permute-start(bf16[2,128,128]{2,1,0:T(8,128)(2,1)S(1)} %pad_maximum_fusion.1), channel_id=1, source_target_pairs={{0,2},{1,3},{2,0},{3,1},{4,6},{5,7},{6,4},{7,5},{8,10},{9,11},{10,... | collective-permute-start | bytes 196616 | tf_op jit(solution)/shard_map/ppermute | solution.py:141
  38.5 4.1 %collective-permute-start.9 = (bf16[2,128,128]{2,1,0:T(8,128)(2,1)S(1)}, bf16[2,128,128]{2,1,0:T(8,128)(2,1)S(1)}, u32[]{:S(2)}, u32[]{:S(2)}) collective-permute-start(bf16[2,128,128]{2,1,0:T(8,128)(2,1)S(1)} %pad_maximum_fusion.2), channel_id=1, source_target_pairs={{0,3},{1,2},{2,1},{3,0},{4,7},{5,6},{6,5},{7,4},{8,11},{9,10},{10,... | collective-permute-start | bytes 196616 | tf_op jit(solution)/shard_map/ppermute | solution.py:141
  38.6 4.1 %collective-permute-start.7 = (bf16[2,128,128]{2,1,0:T(8,128)(2,1)S(1)}, bf16[2,128,128]{2,1,0:T(8,128)(2,1)S(1)}, u32[]{:S(2)}, u32[]{:S(2)}) collective-permute-start(bf16[2,128,128]{2,1,0:T(8,128)(2,1)S(1)} %pad_maximum_fusion), channel_id=1, source_target_pairs={{0,1},{1,0},{2,3},{3,2},{4,5},{5,4},{6,7},{7,6},{8,9},{9,8},{10,11... | collective-permute-start | bytes 196616 | tf_op jit(solution)/shard_map/ppermute | solution.py:141

commit v2 on v1

v2 whole, which is shorter than its diff:
```python
import jax
import jax.numpy as jnp
from jax import lax
from jax.experimental import pallas as pl
from jax.experimental.pallas import tpu as pltpu
from jax.sharding import PartitionSpec as P


GX = "gx"
GY = "gy"


def nt(a, b):
    return lax.dot_general(a, b, (((1,), (1,)), ((), ())), preferred_element_type=jnp.float32)


def nn(a, b):
    return jnp.dot(a, b, preferred_element_type=jnp.float32)


def eliminator_of(interp, redinv, pivot_row, rank):
    width, points = interp.shape
    pivot_col = jnp.transpose(jnp.broadcast_to(pivot_row, (8, width)))[:, :1]
    slot = lax.broadcasted_iota(jnp.int32, (width, points), 0)
    point = lax.broadcasted_iota(jnp.int32, (width, points), 1)
    select = jnp.where((point == pivot_col) & (slot < rank), 1.0, 0.0)
    redundant_row = jnp.sum(select, axis=0, keepdims=True) < 0.5
    slot_t = lax.broadcasted_iota(jnp.int32, (points, width), 1)
    point_t = lax.broadcasted_iota(jnp.int32, (points, width), 0)
    select_t = jnp.where((point_t == pivot_row) & (slot_t < rank), 1.0, 0.0)
    redundant_col = jnp.max(select_t, axis=1, keepdims=True) < 0.5
    coefficients = jnp.where((slot < rank) & redundant_row, interp, jnp.zeros_like(interp))
    half_skel = (-nt(redinv, coefficients)).astype(jnp.bfloat16)
    spread = nn(half_skel, select.astype(jnp.bfloat16)).astype(jnp.bfloat16)
    halfway = jnp.where(redundant_row, redinv, spread)
    elim_skel = (-nn(coefficients, halfway)).astype(jnp.bfloat16)
    spread = nn(select_t.astype(jnp.bfloat16), elim_skel).astype(jnp.bfloat16)
    return jnp.where(redundant_col, halfway, spread)


def fill_table(table, neighbors, box_dev, near_count, lane_count, slots):
    me = lax.axis_index(GX)
    for b in range(box_dev):
        for u in range(slots):
            table[b, u] = near_count
    for b in range(box_dev):
        for n in range(near_count):
            target = neighbors[b, n]
            row = target // (box_dev * lane_count)
            table[b, (row ^ me) * box_dev + target % box_dev] = n


def slot_updates(table, slots, elims, back_v, near_v, lifted_v, near_count, group, store, ready=None):
    box_dev, _, width, _ = back_v.shape
    for first in range(0, len(slots), group):
        these = slots[first : first + group]
        for b in range(box_dev):
            rows = jnp.concatenate([back_v[b, table[b, u]] for u in these], axis=0)
            lifted_v[b, pl.ds(0, len(these) * width)] = nn(rows, elims[b][...]).astype(jnp.bfloat16)
        if ready is not None and first == 0:
            ready()
        for i, u in enumerate(these):
            total = None
            for b in range(box_dev):
                if u != b:
                    n = jnp.minimum(table[b, u], near_count - 1)
                    term = nn(lifted_v[b, pl.ds(i * width, width)], near_v[b, n])
                    total = term if total is None else total + term
            store(first + i, (-total).astype(jnp.bfloat16))


def early_kernel(sizes, early):
    box_dev, near_count, lane_count, slots, group = sizes

    def kernel(ranks_h, neighbors_h, pivots_h, interp_h, redinv_h, back_h, near_h, *rest):
        out, elim_v, ranks, neighbors, pivots, interp_v, redinv_v, back_v, near_v = rest[:9]
        lifted_v, table, few, sems = rest[9:]
        width, points = interp_v.shape[1:]
        heads = [
            pltpu.make_async_copy(neighbors_h, neighbors, few.at[0]),
            pltpu.make_async_copy(ranks_h, ranks, few.at[1]),
            pltpu.make_async_copy(pivots_h, pivots, few.at[2]),
        ]
        copies = []
        for b in range(box_dev):
            copies.append(
                [
                    pltpu.make_async_copy(interp_h.at[b], interp_v.at[b], sems.at[b, 0]),
                    pltpu.make_async_copy(redinv_h.at[b], redinv_v.at[b], sems.at[b, 1]),
                    pltpu.make_async_copy(
                        back_h.at[b], back_v.at[b, pl.ds(0, near_count)], sems.at[b, 2]
                    ),
                    pltpu.make_async_copy(near_h.at[b], near_v.at[b], sems.at[b, 3]),
                ]
            )
        for copy in heads:
            copy.start()
        for b in range(box_dev):
            copies[b][0].start()
            copies[b][1].start()
        for b in range(box_dev):
            back_v[b, near_count] = jnp.zeros((width, points), jnp.bfloat16)
        for copy in heads:
            copy.wait()
        fill_table(table, neighbors, box_dev, near_count, lane_count, slots)
        elims = []
        for b in range(box_dev):
            copies[b][0].wait()
            copies[b][1].wait()
            if b == 0:
                for j in (2, 3):
                    for c in range(box_dev):
                        copies[c][j].start()
        for b in range(box_dev):
            elim_v[b] = eliminator_of(interp_v[b], redinv_v[b], pivots[pl.ds(b, 1), :], ranks[b])
            elims.append(elim_v.at[b])
        for b in range(box_dev):
            copies[b][2].wait()

        def store(i, block):
            out[i] = block

        slot_updates(table, early, elims, back_v, near_v, lifted_v, near_count, group, store, lambda: [copies[b][3].wait() for b in range(box_dev)])

    return kernel


def late_kernel(sizes, late, splits):
    box_dev, near_count, lane_count, slots = sizes[:4]

    def kernel(neighbors_h, back_h, near_h, elim_v, *rest):
        outs = rest[:-8]
        neighbors, back_v, near_v, lifted_v, table, few, back_sems, near_sems = rest[-8:]
        width, points = back_v.shape[2:]
        head = pltpu.make_async_copy(neighbors_h, neighbors, few.at[0])
        head.start()
        spans = [pl.ds(first, count) for first, count in splits]
        back_copies = [
            [
                pltpu.make_async_copy(
                    back_h.at[b, span], back_v.at[b, span], back_sems.at[b, i]
                )
                for b in range(box_dev)
            ]
            for i, span in enumerate(spans)
        ]
        near_copies = [
            pltpu.make_async_copy(near_h.at[b], near_v.at[b], near_sems.at[b])
            for b in range(box_dev)
        ]
        for copies in back_copies + [near_copies]:
            for copy in copies:
                copy.start()
        for b in range(box_dev):
            lifted_v[b, near_count] = jnp.zeros((width, points), jnp.bfloat16)
        head.wait()
        fill_table(table, neighbors, box_dev, near_count, lane_count, slots)
        for (first, count), span, copies in zip(splits, spans, back_copies):
            for copy in copies:
                copy.wait()
            for b in range(box_dev):
                rows = back_v[b, span].reshape(count * width, points)
                lifted = nn(rows, elim_v[b]).astype(jnp.bfloat16)
                lifted_v[b, span] = lifted.reshape(count, width, points)
        for copy in near_copies:
            copy.wait()
        for i, u in enumerate(late):
            total = None
            for b in range(box_dev):
                if u != b:
                    n = table[b, u]
                    term = nn(lifted_v[b, n], near_v[b, jnp.minimum(n, near_count - 1)])
                    total = term if total is None else total + term
            outs[i // box_dev][i % box_dev] = (-total).astype(jnp.bfloat16)

    return kernel


def in_hbm(*values):
    return [pltpu.with_memory_space_constraint(v, pltpu.HBM) for v in values]


def swap(value, axis, size, k):
    return lax.ppermute(value, axis, [(a, a ^ k) for a in range(size)])


def layer(self_blk, near, back, interp, redinv, ranks, pivots, neighbors, parent):
    gx_count = lax.axis_size(GX)
    lane_count = lax.axis_size(GY)
    box_dev, near_count, points, width = near.shape
    bf16 = jnp.bfloat16
    half, quarter = gx_count // 2, gx_count // 4
    early_k = [half + quarter + j for j in range(quarter)]
    late_k = [half + j for j in range(quarter)] + list(range(half))
    group = 4
    sizes = (box_dev, near_count, lane_count, gx_count * box_dev, group)
    slots_of = lambda ks: [k * box_dev + s for k in ks for s in range(box_dev)]
    hbm = pl.BlockSpec(memory_space=pltpu.HBM)
    vmem = pl.BlockSpec(memory_space=pltpu.VMEM)
    table = pltpu.SMEM((box_dev, gx_count * box_dev), jnp.int32)
    params = pltpu.CompilerParams(vmem_limit_bytes=24 * 1024 * 1024)
    early, elim = pl.pallas_call(
        early_kernel(sizes, slots_of(early_k)),
        out_shape=[
            jax.ShapeDtypeStruct((len(early_k) * box_dev, width, width), bf16),
            jax.ShapeDtypeStruct((box_dev, points, points), bf16),
        ],
        in_specs=[hbm] * 7,
        out_specs=[vmem] * 2,
        scratch_shapes=[
            pltpu.SMEM((box_dev,), jnp.int32),
            pltpu.SMEM((box_dev, near_count), jnp.int32),
            pltpu.VMEM((box_dev, width), jnp.int32),
            pltpu.VMEM(interp.shape, bf16),
            pltpu.VMEM(redinv.shape, bf16),
            pltpu.VMEM((box_dev, near_count + 1, width, points), bf16),
            pltpu.VMEM(near.shape, bf16),
            pltpu.VMEM((box_dev, group * width, points), bf16),
            table,
            pltpu.SemaphoreType.DMA((3,)),
            pltpu.SemaphoreType.DMA((box_dev, 4)),
        ],
        compiler_params=params,
        name="early",
    )(*in_hbm(ranks, neighbors, pivots, interp, redinv, back, near))
    joined = swap(early, GX, gx_count, quarter)
    split = near_count // 2
    splits = [(0, split), (split, near_count - split)]
    late = pl.pallas_call(
        late_kernel(sizes, slots_of(late_k), splits),
        out_shape=[jax.ShapeDtypeStruct((box_dev, width, width), bf16)] * len(late_k),
        in_specs=[hbm] * 3 + [vmem],
        out_specs=[vmem] * len(late_k),
        scratch_shapes=[
            pltpu.SMEM((box_dev, near_count), jnp.int32),
            pltpu.VMEM(back.shape, bf16),
            pltpu.VMEM(near.shape, bf16),
            pltpu.VMEM((box_dev, near_count + 1, width, points), bf16),
            table,
            pltpu.SemaphoreType.DMA((1,)),
            pltpu.SemaphoreType.DMA((box_dev, len(splits))),
            pltpu.SemaphoreType.DMA((box_dev,)),
        ],
        compiler_params=params,
        name="late",
    )(*in_hbm(neighbors, back, near), elim)
    part = dict(zip(late_k, late))
    summed = part[0].astype(jnp.float32)
    for j in reversed(range(quarter)):
        k = half + j
        added = joined[j * box_dev : (j + 1) * box_dev].astype(jnp.float32)
        block = (part[k].astype(jnp.float32) + added).astype(bf16)
        summed += swap(block, GX, gx_count, k).astype(jnp.float32)
    for k in reversed(range(1, half)):
        summed += swap(part[k], GX, gx_count, k).astype(jnp.float32)
    living = jnp.arange(width, dtype=jnp.int32)[None, :] < ranks[:, None]
    masking = living[:, :, None] & living[:, None, :]
    merged = jnp.where(masking, self_blk + summed, 0.0)
    row = parent - lax.axis_index(GX) * (lane_count * box_dev)
    lane = lax.axis_index(GY)
    result = None
    for k in range(lane_count):
        rows = []
        for s in range(box_dev):
            here = row == (lane ^ k) * box_dev + s
            rows.append(jnp.sum(jnp.where(here[:, None, None], merged, 0.0), axis=0))
        placed = jnp.stack(rows)
        if k:
            placed = swap(placed.astype(bf16), GY, lane_count, k).astype(jnp.float32)
        result = placed if result is None else result + placed
    return result


def solution(mesh):
    split = (GX, GY)
    placed = (
        P(split, None, None),
        P(split, None, None, None),
        P(split, None, None, None),
        P(split, None, None),
        P(split, None, None),
        P(split),
        P(split, None),
        P(split, None),
        P(split),
    )
    return jax.shard_map(
        layer, mesh=mesh, in_specs=placed, out_specs=P(split, None, None), check_vma=False
    )
```

time: 43.6 us -> 37.3 us (0.86)
  local copies, waits for them, and re-layouts: 8.27 us -> 0.02 us
  waiting for transfers between devices: 10.3 us -> 14.6 us
  starting transfers between devices: 14.9 us -> 11.9 us
  Pallas kernels: 8.76 us -> 9.53 us
    unnamed x20 -> x6, local copies, waits for them, and re-layouts: 8.27 us -> 0.02 us
    ppermute x10 -> x9, waiting for transfers between devices: 10.3 us -> 14.6 us  [swap(): return lax.ppermute(value, axis, [(a, a ^ k) for a in range(size)])]
    ppermute x10 -> x9, starting transfers between devices: 14.9 us -> 11.9 us  [swap(): return lax.ppermute(value, axis, [(a, a ^ k) for a in range(size)])]
    pallas_call x1 -> x2, Pallas kernels: 8.76 us -> 9.53 us  [the longest x1 4.82 us: layer(): pl.pallas_call(early_kernel(sizes, slots_of(early_k)), out_shape=[jax.Sha...]
  transfers between devices with their start and end apart: 10 -> 9, of which waited for: 4 -> 5; matrix products, arithmetic and copies ran while one was open for 0% -> 0% of each run, Pallas kernels for 0% -> 0%
where the time goes in v2:
time: 37.3 us; the launch traced here: 37.1 us
  waiting for transfers between devices  14.6 us (39%)
  starting transfers between devices  11.9 us (32%)
  Pallas kernels  9.53 us (26%)
  other arithmetic  1 us (3%)
    ppermute x9, waiting for transfers between devices, swap(): return lax.ppermute(value, axis, [(a, a ^ k) for a in range(size)])  14.6 us
    ppermute x9, starting transfers between devices, swap(): return lax.ppermute(value, axis, [(a, a ^ k) for a in range(size)])  11.9 us
    pallas_call x1, Pallas kernels, layer(): pl.pallas_call(early_kernel(sizes, slots_of(early_k)), out_shape=[jax.Sha...  4.82 us
    pallas_call x1, Pallas kernels, layer(): pl.pallas_call(late_kernel(sizes, slots_of(late_k), splits), out_shape=[j...  4.71 us
  transfers between devices with their start and end apart: 9, of which 5 were waited for; matrix products, arithmetic and copies ran while one was open for 0% of the time, Pallas kernels for 0%

profile of v2, /device:TPU:0, one launch (start us, length us, event | category | flops | bytes accessed | tf_op | source)
XLA Modules:
  0.0 37.1 jit_solution(18175152774702259097)
XLA Ops:
  0.0 4.8 %early.1 = (bf16[4,128,128]{2,1,0:T(8,128)(2,1)S(1)}, bf16[2,512,512]{2,1,0:T(8,128)(2,1)S(1)}) custom-call(s32[2]{0:T(128)} %ranks_h.1, s32[2,14]{1,0:T(2,128)} %neighbors_h.3, s32[2,128]{1,0:T(2,128)} %pivots_h.1, bf16[2,128,512]{2,1,0:T(8,128)(2,1)} %interp_h.1, bf16[2,512,512]{2,1,0:T(8,128)(2,1)} %redinv_h.1, bf16[2,14,128,512]{3,2,1,0:T(8,128)(2,1)} %back_h.3, ...), custom_call_target="tpu_custom_call" | custom-call | tf_op jit(solution)/shard_map/early/pallas_call | solution.py:202
  4.8 0.0 copy-start.2
  4.8 0.0 copy-start.1
  4.9 0.0 copy-start
  4.9 4.7 %late.1 = (bf16[2,128,128]{2,1,0:T(8,128)(2,1)S(1)}, bf16[2,128,128]{2,1,0:T(8,128)(2,1)S(1)}, bf16[2,128,128]{2,1,0:T(8,128)(2,1)S(1)}, bf16[2,128,128]{2,1,0:T...) custom-call(s32[2,14]{1,0:T(2,128)} %neighbors_h.3, ...), custom_call_target="tpu_custom_call" | custom-call | tf_op jit(solution)/shard_map/late/pallas_call | solution.py:229
  9.6 3.0 %collective-permute-start.5 = (bf16[2,128,128]{2,1,0:T(8,128)(2,1)S(1)}, bf16[2,128,128]{2,1,0:T(8,128)(2,1)S(1)}, u32[]{:S(2)}, u32[]{:S(2)}) collective-permute-start(bf16[2,128,128]{2,1,0:T(8,128)(2,1)S(1)} %get-tuple-element.20), channel_id=1, source_target_pairs={{0,4},{4,0},{8,12},{12,8},{16,20},{20,16},{24,28},{28,24},{1,5},{5... | collective-permute-start | bytes 196616 | tf_op jit(solution)/shard_map/ppermute | solution.py:184
  12.6 1.6 %collective-permute-start.4 = (bf16[2,128,128]{2,1,0:T(8,128)(2,1)S(1)}, bf16[2,128,128]{2,1,0:T(8,128)(2,1)S(1)}, u32[]{:S(2)}, u32[]{:S(2)}) collective-permute-start(bf16[2,128,128]{2,1,0:T(8,128)(2,1)S(1)} %get-tuple-element.19), channel_id=1, source_target_pairs={{0,8},{4,12},{8,0},{12,4},{16,24},{20,28},{24,16},{28,20},{1,9},{5... | collective-permute-start | bytes 196616 | tf_op jit(solution)/shard_map/ppermute | solution.py:184
  14.2 0.0 collective-permute-start.3
  14.2 2.0 %collective-permute-start = (bf16[4,128,128]{2,1,0:T(8,128)(2,1)S(1)}, bf16[4,128,128]{2,1,0:T(8,128)(2,1)S(1)}, u32[]{:S(2)}, u32[]{:S(2)}) collective-permute-start(bf16[4,128,128]{2,1,0:T(8,128)(2,1)S(1)} %get-tuple-element.16), channel_id=1, source_target_pairs={{0,8},{4,12},{8,0},{12,4},{16,24},{20,28},{24,16},{28,20},{1,9},{5... | collective-permute-start | bytes 393224 | tf_op jit(solution)/shard_map/ppermute | solution.py:184
  16.2 4.7 %collective-permute-done = bf16[4,128,128]{2,1,0:T(8,128)(2,1)S(1)} collective-permute-done((bf16[4,128,128]{2,1,0:T(8,128)(2,1)S(1)}, bf16[4,128,128]{2,1,0:T(8,128)(2,1)S(1)}, u32[]{:S(2)}, u32[]{:S(2)}) %collective-permute-start) | collective-permute-done | bytes 131104 | tf_op jit(solution)/shard_map/ppermute | solution.py:184
  21.0 2.7 %collective-permute-start.2 = (bf16[2,128,128]{2,1,0:T(8,128)(2,1)S(1)}, bf16[2,128,128]{2,1,0:T(8,128)(2,1)S(1)}, u32[]{:S(2)}, u32[]{:S(2)}) collective-permute-start(bf16[2,128,128]{2,1,0:T(8,128)(2,1)S(1)} %get-tuple-element.32), channel_id=1, source_target_pairs={{0,16},{4,20},{8,24},{12,28},{16,0},{20,4},{24,8},{28,12},{1,17},{... | collective-permute-start | bytes 196616 | tf_op jit(solution)/shard_map/ppermute | solution.py:184
  23.6 0.6 %collective-permute-start.1 = (bf16[2,128,128]{2,1,0:T(8,128)(2,1)S(1)}, bf16[2,128,128]{2,1,0:T(8,128)(2,1)S(1)}, u32[]{:S(2)}, u32[]{:S(2)}) collective-permute-start(bf16[2,128,128]{2,1,0:T(8,128)(2,1)S(1)} %get-tuple-element.31), channel_id=1, source_target_pairs={{0,20},{4,16},{8,28},{12,24},{16,4},{20,0},{24,12},{28,8},{1,21},{... | collective-permute-start | bytes 196616 | tf_op jit(solution)/shard_map/ppermute | solution.py:184
  24.2 0.1 iota_compare_fusion
  24.3 0.0 collective-permute-done.3
  24.3 4.0 %collective-permute-done.2 = bf16[2,128,128]{2,1,0:T(8,128)(2,1)S(1)} collective-permute-done((bf16[2,128,128]{2,1,0:T(8,128)(2,1)S(1)}, bf16[2,128,128]{2,1,0:T(8,128)(2,1)S(1)}, u32[]{:S(2)}, u32[]{:S(2)}) %collective-permute-start.2) | collective-permute-done | bytes 65568 | tf_op jit(solution)/shard_map/ppermute | solution.py:184
  28.3 2.1 %collective-permute-done.1 = bf16[2,128,128]{2,1,0:T(8,128)(2,1)S(1)} collective-permute-done((bf16[2,128,128]{2,1,0:T(8,128)(2,1)S(1)}, bf16[2,128,128]{2,1,0:T(8,128)(2,1)S(1)}, u32[]{:S(2)}, u32[]{:S(2)}) %collective-permute-start.1) | collective-permute-done | bytes 65568 | tf_op jit(solution)/shard_map/ppermute | solution.py:184
  30.4 0.2 select_reduce_fusion.5
  30.6 0.1 collective-permute-start.8
  30.7 1.6 %collective-permute-start.7 = (bf16[2,128,128]{2,1,0:T(8,128)(2,1)S(1)}, bf16[2,128,128]{2,1,0:T(8,128)(2,1)S(1)}, u32[]{:S(2)}, u32[]{:S(2)}) collective-permute-start(bf16[2,128,128]{2,1,0:T(8,128)(2,1)S(1)} %pad_maximum_fusion.1), channel_id=1, source_target_pairs={{0,2},{1,3},{2,0},{3,1},{4,6},{5,7},{6,4},{7,5},{8,10},{9,11},{10,... | collective-permute-start | bytes 196616 | tf_op jit(solution)/shard_map/ppermute | solution.py:184
  32.3 0.4 %collective-permute-start.6 = (bf16[2,128,128]{2,1,0:T(8,128)(2,1)S(1)}, bf16[2,128,128]{2,1,0:T(8,128)(2,1)S(1)}, u32[]{:S(2)}, u32[]{:S(2)}) collective-permute-start(bf16[2,128,128]{2,1,0:T(8,128)(2,1)S(1)} %pad_maximum_fusion), channel_id=1, source_target_pairs={{0,1},{1,0},{2,3},{3,2},{4,5},{5,4},{6,7},{7,6},{8,9},{9,8},{10,11... | collective-permute-start | bytes 196616 | tf_op jit(solution)/shard_map/ppermute | solution.py:184
  32.7 2.3 %collective-permute-done.8 = bf16[2,128,128]{2,1,0:T(8,128)(2,1)S(1)} collective-permute-done((bf16[2,128,128]{2,1,0:T(8,128)(2,1)S(1)}, bf16[2,128,128]{2,1,0:T(8,128)(2,1)S(1)}, u32[]{:S(2)}, u32[]{:S(2)}) %collective-permute-start.8) | collective-permute-done | bytes 65568 | tf_op jit(solution)/shard_map/ppermute | solution.py:184
  35.0 1.5 %collective-permute-done.7 = bf16[2,128,128]{2,1,0:T(8,128)(2,1)S(1)} collective-permute-done((bf16[2,128,128]{2,1,0:T(8,128)(2,1)S(1)}, bf16[2,128,128]{2,1,0:T(8,128)(2,1)S(1)}, u32[]{:S(2)}, u32[]{:S(2)}) %collective-permute-start.7) | collective-permute-done | bytes 65568 | tf_op jit(solution)/shard_map/ppermute | solution.py:184
  36.5 0.0 collective-permute-done.6
  36.5 0.7 %fusion.1 = f32[2,128,128]{2,1,0:T(8,128)} fusion(f32[1,128,128]{2,1,0:T(8,128)S(1)} %bitcast.20, f32[1,128,128]{2,1,0:T(8,128)S(1)} %bitcast.21, bf16[2,128,128]{2,1,0:T(8,128)(2,1)S(1)} %collective-permute-done.8, bf16[2,128,128]{2,1,0:T(8,128)(2,1)S(1)} %collective-permute-done.7, bf16[2,128,128]{2,1,0:T(8,128)(2,1)S(1)} %collective-permute-done.6), kind=kLoop, calls=%fused_computation.2 | loop fusion | flops 229376 | bytes 458752 | tf_op jit(solution)/shard_map/add | solution.py:270
  (11 shorter events, 0.1 us)
Async XLA Ops:
  4.8 11.4 %copy-start.2 = (s32[2]{0:T(128)S(1)}, s32[2]{0:T(128)}, u32[]{:S(2)}) copy-start(s32[2]{0:T(128)} %param.17) | copy-start | bytes 28
  4.8 19.4 %copy-start.1 = (s32[2]{0:T(128)S(1)}, s32[2]{0:T(128)}, u32[]{:S(2)}) copy-start(s32[2]{0:T(128)} %ranks_h.1) | copy-start | bytes 28
  4.9 25.6 %copy-start = (f32[2,128,128]{2,1,0:T(8,128)S(1)}, f32[2,128,128]{2,1,0:T(8,128)}, u32[]{:S(2)}) copy-start(f32[2,128,128]{2,1,0:T(8,128)} %param.9) | copy-start | bytes 393220
  9.6 14.7 %collective-permute-start.5 = (bf16[2,128,128]{2,1,0:T(8,128)(2,1)S(1)}, bf16[2,128,128]{2,1,0:T(8,128)(2,1)S(1)}, u32[]{:S(2)}, u32[]{:S(2)}) collective-permute-start(bf16[2,128,128]{2,1,0:T(8,128)(2,1)S(1)} %get-tuple-element.20), channel_id=1, source_target_pairs={{0,4},{4,0},{8,12},{12,8},{16,20},{20,16},{24,28},{28,24},{1,5},{5... | collective-permute-start | bytes 196616 | tf_op jit(solution)/shard_map/ppermute | solution.py:184
  12.6 11.7 %collective-permute-start.4 = (bf16[2,128,128]{2,1,0:T(8,128)(2,1)S(1)}, bf16[2,128,128]{2,1,0:T(8,128)(2,1)S(1)}, u32[]{:S(2)}, u32[]{:S(2)}) collective-permute-start(bf16[2,128,128]{2,1,0:T(8,128)(2,1)S(1)} %get-tuple-element.19), channel_id=1, source_target_pairs={{0,8},{4,12},{8,0},{12,4},{16,24},{20,28},{24,16},{28,20},{1,9},{5... | collective-permute-start | bytes 196616 | tf_op jit(solution)/shard_map/ppermute | solution.py:184
  14.2 10.1 %collective-permute-start.3 = (bf16[2,128,128]{2,1,0:T(8,128)(2,1)S(1)}, bf16[2,128,128]{2,1,0:T(8,128)(2,1)S(1)}, u32[]{:S(2)}, u32[]{:S(2)}) collective-permute-start(bf16[2,128,128]{2,1,0:T(8,128)(2,1)S(1)} %get-tuple-element.18), channel_id=1, source_target_pairs={{0,12},{4,8},{8,4},{12,0},{16,28},{20,24},{24,20},{28,16},{1,13},{... | collective-permute-start | bytes 196616 | tf_op jit(solution)/shard_map/ppermute | solution.py:184
  14.2 6.8 %collective-permute-start = (bf16[4,128,128]{2,1,0:T(8,128)(2,1)S(1)}, bf16[4,128,128]{2,1,0:T(8,128)(2,1)S(1)}, u32[]{:S(2)}, u32[]{:S(2)}) collective-permute-start(bf16[4,128,128]{2,1,0:T(8,128)(2,1)S(1)} %get-tuple-element.16), channel_id=1, source_target_pairs={{0,8},{4,12},{8,0},{12,4},{16,24},{20,28},{24,16},{28,20},{1,9},{5... | collective-permute-start | bytes 393224 | tf_op jit(solution)/shard_map/ppermute | solution.py:184
  21.0 7.3 %collective-permute-start.2 = (bf16[2,128,128]{2,1,0:T(8,128)(2,1)S(1)}, bf16[2,128,128]{2,1,0:T(8,128)(2,1)S(1)}, u32[]{:S(2)}, u32[]{:S(2)}) collective-permute-start(bf16[2,128,128]{2,1,0:T(8,128)(2,1)S(1)} %get-tuple-element.32), channel_id=1, source_target_pairs={{0,16},{4,20},{8,24},{12,28},{16,0},{20,4},{24,8},{28,12},{1,17},{... | collective-permute-start | bytes 196616 | tf_op jit(solution)/shard_map/ppermute | solution.py:184
  23.6 6.8 %collective-permute-start.1 = (bf16[2,128,128]{2,1,0:T(8,128)(2,1)S(1)}, bf16[2,128,128]{2,1,0:T(8,128)(2,1)S(1)}, u32[]{:S(2)}, u32[]{:S(2)}) collective-permute-start(bf16[2,128,128]{2,1,0:T(8,128)(2,1)S(1)} %get-tuple-element.31), channel_id=1, source_target_pairs={{0,20},{4,16},{8,28},{12,24},{16,4},{20,0},{24,12},{28,8},{1,21},{... | collective-permute-start | bytes 196616 | tf_op jit(solution)/shard_map/ppermute | solution.py:184
  30.6 4.4 %collective-permute-start.8 = (bf16[2,128,128]{2,1,0:T(8,128)(2,1)S(1)}, bf16[2,128,128]{2,1,0:T(8,128)(2,1)S(1)}, u32[]{:S(2)}, u32[]{:S(2)}) collective-permute-start(bf16[2,128,128]{2,1,0:T(8,128)(2,1)S(1)} %pad_maximum_fusion.2), channel_id=1, source_target_pairs={{0,3},{1,2},{2,1},{3,0},{4,7},{5,6},{6,5},{7,4},{8,11},{9,10},{10,... | collective-permute-start | bytes 196616 | tf_op jit(solution)/shard_map/ppermute | solution.py:184
  30.7 5.8 %collective-permute-start.7 = (bf16[2,128,128]{2,1,0:T(8,128)(2,1)S(1)}, bf16[2,128,128]{2,1,0:T(8,128)(2,1)S(1)}, u32[]{:S(2)}, u32[]{:S(2)}) collective-permute-start(bf16[2,128,128]{2,1,0:T(8,128)(2,1)S(1)} %pad_maximum_fusion.1), channel_id=1, source_target_pairs={{0,2},{1,3},{2,0},{3,1},{4,6},{5,7},{6,4},{7,5},{8,10},{9,11},{10,... | collective-permute-start | bytes 196616 | tf_op jit(solution)/shard_map/ppermute | solution.py:184
  32.3 4.2 %collective-permute-start.6 = (bf16[2,128,128]{2,1,0:T(8,128)(2,1)S(1)}, bf16[2,128,128]{2,1,0:T(8,128)(2,1)S(1)}, u32[]{:S(2)}, u32[]{:S(2)}) collective-permute-start(bf16[2,128,128]{2,1,0:T(8,128)(2,1)S(1)} %pad_maximum_fusion), channel_id=1, source_target_pairs={{0,1},{1,0},{2,3},{3,2},{4,5},{5,4},{6,7},{7,6},{8,9},{9,8},{10,11... | collective-permute-start | bytes 196616 | tf_op jit(solution)/shard_map/ppermute | solution.py:184

commit v3 on v2

--- a/solution.py
+++ b/solution.py
@@ -73,8 +73,9 @@
     box_dev, near_count, lane_count, slots, group = sizes
 
     def kernel(ranks_h, neighbors_h, pivots_h, interp_h, redinv_h, back_h, near_h, *rest):
-        out, elim_v, ranks, neighbors, pivots, interp_v, redinv_v, back_v, near_v = rest[:9]
-        lifted_v, table, few, sems = rest[9:]
+        outs, elim_v = rest[:-12], rest[-12]
+        ranks, neighbors, pivots, interp_v, redinv_v, back_v, near_v = rest[-11:-4]
+        lifted_v, table, few, sems = rest[-4:]
         width, points = interp_v.shape[1:]
         heads = [
             pltpu.make_async_copy(neighbors_h, neighbors, few.at[0]),
@@ -118,59 +119,43 @@
             copies[b][2].wait()
 
         def store(i, block):
-            out[i] = block
+            outs[i // group][i % group] = block
 
         slot_updates(table, early, elims, back_v, near_v, lifted_v, near_count, group, store, lambda: [copies[b][3].wait() for b in range(box_dev)])
 
     return kernel
 
 
-def late_kernel(sizes, late, splits):
+def late_kernel(sizes, late):
     box_dev, near_count, lane_count, slots = sizes[:4]
 
     def kernel(neighbors_h, back_h, near_h, elim_v, *rest):
-        outs = rest[:-8]
-        neighbors, back_v, near_v, lifted_v, table, few, back_sems, near_sems = rest[-8:]
+        outs = rest[:-6]
+        neighbors, back_v, near_v, table, few, sems = rest[-6:]
         width, points = back_v.shape[2:]
         head = pltpu.make_async_copy(neighbors_h, neighbors, few.at[0])
         head.start()
-        spans = [pl.ds(first, count) for first, count in splits]
-        back_copies = [
-            [
-                pltpu.make_async_copy(
-                    back_h.at[b, span], back_v.at[b, span], back_sems.at[b, i]
-                )
-                for b in range(box_dev)
-            ]
-            for i, span in enumerate(spans)
-        ]
-        near_copies = [
-            pltpu.make_async_copy(near_h.at[b], near_v.at[b], near_sems.at[b])
-            for b in range(box_dev)
-        ]
-        for copies in back_copies + [near_copies]:
-            for copy in copies:
-                copy.start()
-        for b in range(box_dev):
-            lifted_v[b, near_count] = jnp.zeros((width, points), jnp.bfloat16)
         head.wait()
         fill_table(table, neighbors, box_dev, near_count, lane_count, slots)
-        for (first, count), span, copies in zip(splits, spans, back_copies):
-            for copy in copies:
-                copy.wait()
+        copies = []
+        for b in range(box_dev):
+            for i, u in enumerate(late):
+                n = jnp.minimum(table[b, u], near_count - 1)
+                copies.append(pltpu.make_async_copy(back_h.at[b, n], back_v.at[b, i], sems.at[0, b, i]))
+                copies.append(pltpu.make_async_copy(near_h.at[b, n], near_v.at[b, i], sems.at[1, b, i]))
+        for copy in copies:
+            copy.start()
+        for copy in copies:
+            copy.wait()
+        lifted = []
+        for b in range(box_dev):
+            rows = back_v[b].reshape(len(late) * width, points)
+            lifted.append(nn(rows, elim_v[b]).astype(jnp.bfloat16))
+        for i, u in enumerate(late):
+            total = jnp.zeros((width, width), jnp.float32)
             for b in range(box_dev):
-                rows = back_v[b, span].reshape(count * width, points)
-                lifted = nn(rows, elim_v[b]).astype(jnp.bfloat16)
-                lifted_v[b, span] = lifted.reshape(count, width, points)
-        for copy in near_copies:
-            copy.wait()
-        for i, u in enumerate(late):
-            total = None
-            for b in range(box_dev):
-                if u != b:
-                    n = table[b, u]
-                    term = nn(lifted_v[b, n], near_v[b, jnp.minimum(n, near_count - 1)])
-                    total = term if total is None else total + term
+                term = nn(lifted[b][i * width : (i + 1) * width], near_v[b, i])
+                total += jnp.where(table[b, u] < near_count, term, 0.0)
             outs[i // box_dev][i % box_dev] = (-total).astype(jnp.bfloat16)
 
     return kernel
@@ -189,24 +174,23 @@
     lane_count = lax.axis_size(GY)
     box_dev, near_count, points, width = near.shape
     bf16 = jnp.bfloat16
-    half, quarter = gx_count // 2, gx_count // 4
-    early_k = [half + quarter + j for j in range(quarter)]
-    late_k = [half + j for j in range(quarter)] + list(range(half))
-    group = 4
+    half = gx_count // 2
+    peers = range(1, half)
+    early_k = [k for j in peers for k in (half + j, j)]
+    late_k = [half, 0]
+    group = 2 * box_dev
     sizes = (box_dev, near_count, lane_count, gx_count * box_dev, group)
     slots_of = lambda ks: [k * box_dev + s for k in ks for s in range(box_dev)]
     hbm = pl.BlockSpec(memory_space=pltpu.HBM)
     vmem = pl.BlockSpec(memory_space=pltpu.VMEM)
     table = pltpu.SMEM((box_dev, gx_count * box_dev), jnp.int32)
     params = pltpu.CompilerParams(vmem_limit_bytes=24 * 1024 * 1024)
-    early, elim = pl.pallas_call(
+    *early, elim = pl.pallas_call(
         early_kernel(sizes, slots_of(early_k)),
-        out_shape=[
-            jax.ShapeDtypeStruct((len(early_k) * box_dev, width, width), bf16),
-            jax.ShapeDtypeStruct((box_dev, points, points), bf16),
-        ],
+        out_shape=[jax.ShapeDtypeStruct((group, width, width), bf16)] * len(peers)
+        + [jax.ShapeDtypeStruct((box_dev, points, points), bf16)],
         in_specs=[hbm] * 7,
-        out_specs=[vmem] * 2,
+        out_specs=[vmem] * (len(peers) + 1),
         scratch_shapes=[
             pltpu.SMEM((box_dev,), jnp.int32),
             pltpu.SMEM((box_dev, near_count), jnp.int32),
@@ -223,36 +207,27 @@
         compiler_params=params,
         name="early",
     )(*in_hbm(ranks, neighbors, pivots, interp, redinv, back, near))
-    joined = swap(early, GX, gx_count, quarter)
-    split = near_count // 2
-    splits = [(0, split), (split, near_count - split)]
-    late = pl.pallas_call(
-        late_kernel(sizes, slots_of(late_k), splits),
-        out_shape=[jax.ShapeDtypeStruct((box_dev, width, width), bf16)] * len(late_k),
+    joined = [swap(sent, GX, gx_count, j) for j, sent in zip(peers, early)]
+    far, close = pl.pallas_call(
+        late_kernel(sizes, slots_of(late_k)),
+        out_shape=[jax.ShapeDtypeStruct((box_dev, width, width), bf16)] * 2,
         in_specs=[hbm] * 3 + [vmem],
-        out_specs=[vmem] * len(late_k),
+        out_specs=[vmem] * 2,
         scratch_shapes=[
             pltpu.SMEM((box_dev, near_count), jnp.int32),
-            pltpu.VMEM(back.shape, bf16),
-            pltpu.VMEM(near.shape, bf16),
-            pltpu.VMEM((box_dev, near_count + 1, width, points), bf16),
+            pltpu.VMEM((box_dev, len(late_k) * box_dev, width, points), bf16),
+            pltpu.VMEM((box_dev, len(late_k) * box_dev, points, width), bf16),
             table,
             pltpu.SemaphoreType.DMA((1,)),
-            pltpu.SemaphoreType.DMA((box_dev, len(splits))),
-            pltpu.SemaphoreType.DMA((box_dev,)),
+            pltpu.SemaphoreType.DMA((2, box_dev, len(late_k) * box_dev)),
         ],
         compiler_params=params,
         name="late",
     )(*in_hbm(neighbors, back, near), elim)
-    part = dict(zip(late_k, late))
-    summed = part[0].astype(jnp.float32)
-    for j in reversed(range(quarter)):
-        k = half + j
-        added = joined[j * box_dev : (j + 1) * box_dev].astype(jnp.float32)
-        block = (part[k].astype(jnp.float32) + added).astype(bf16)
-        summed += swap(block, GX, gx_count, k).astype(jnp.float32)
-    for k in reversed(range(1, half)):
-        summed += swap(part[k], GX, gx_count, k).astype(jnp.float32)
+    joined = [part.astype(jnp.float32) for part in joined]
+    far = sum([part[:box_dev] for part in joined], far.astype(jnp.float32)).astype(bf16)
+    summed = sum([part[box_dev:] for part in joined], close.astype(jnp.float32))
+    summed += swap(far, GX, gx_count, half).astype(jnp.float32)
     living = jnp.arange(width, dtype=jnp.int32)[None, :] < ranks[:, None]
     masking = living[:, :, None] & living[:, None, :]
     merged = jnp.where(masking, self_blk + summed, 0.0)
@@ -284,6 +259,4 @@
         P(split, None),
         P(split),
     )
-    return jax.shard_map(
-        layer, mesh=mesh, in_specs=placed, out_specs=P(split, None, None), check_vma=False
-    )
+    return jax.shard_map(layer, mesh=mesh, in_specs=placed, out_specs=P(split, None, None), check_vma=False)

time: 37.3 us -> 29.2 us (0.78)
  waiting for transfers between devices: 14.6 us -> 7.76 us
  starting transfers between devices: 11.9 us -> 9.75 us
  Pallas kernels: 9.53 us -> 10.3 us
    ppermute x9 -> x7, waiting for transfers between devices: 14.6 us -> 7.76 us  [swap(): return lax.ppermute(value, axis, [(a, a ^ k) for a in range(size)])]
    ppermute x9 -> x7, starting transfers between devices: 11.9 us -> 9.75 us  [swap(): return lax.ppermute(value, axis, [(a, a ^ k) for a in range(size)])]
    pallas_call x1, Pallas kernels: 4.82 us -> 6.48 us  [layer(): pl.pallas_call(early_kernel(sizes, slots_of(early_k)), out_shape=[jax.Sha...]
    pallas_call x1, Pallas kernels: 4.71 us -> 3.81 us  [layer(): pl.pallas_call(late_kernel(sizes, slots_of(late_k)), out_shape=[jax.Shape...]
  transfers between devices with their start and end apart: 9 -> 7, of which waited for: 5 -> 5; matrix products, arithmetic and copies ran while one was open for 0% -> 1% of each run, Pallas kernels for 0% -> 13%
where the time goes in v3:
time: 29.2 us; the launch traced here: 29 us
  Pallas kernels  10.3 us (35%)
  starting transfers between devices  9.75 us (33%)
  waiting for transfers between devices  7.76 us (27%)
  other arithmetic  1.07 us (4%)
    ppermute x7, starting transfers between devices, swap(): return lax.ppermute(value, axis, [(a, a ^ k) for a in range(size)])  9.75 us
    ppermute x7, waiting for transfers between devices, swap(): return lax.ppermute(value, axis, [(a, a ^ k) for a in range(size)])  7.76 us
    pallas_call x1, Pallas kernels, layer(): pl.pallas_call(early_kernel(sizes, slots_of(early_k)), out_shape=[jax.Sha...  6.48 us
    pallas_call x1, Pallas kernels, layer(): pl.pallas_call(late_kernel(sizes, slots_of(late_k)), out_shape=[jax.Shape...  3.81 us
    add x1, other arithmetic, layer(): result = placed if result is None else result + placed  0.69 us
  transfers between devices with their start and end apart: 7, of which 5 were waited for; matrix products, arithmetic and copies ran while one was open for 1% of the time, Pallas kernels for 13%

profile of v3, /device:TPU:0, one launch (start us, length us, event | category | flops | bytes accessed | tf_op | source)
XLA Modules:
  0.0 29.0 jit_solution(10839068685840653423)
XLA Ops:
  0.0 6.5 %early.1 = (bf16[4,128,128]{2,1,0:T(8,128)(2,1)S(1)}, bf16[4,128,128]{2,1,0:T(8,128)(2,1)S(1)}, bf16[4,128,128]{2,1,0:T(8,128)(2,1)S(1)}, bf16[2,512,512]{2,1,0:T(8,128)(2,1)S(1)}) custom-call(s32[2]{0:T(128)} %ranks_h.1, s32[2,14]{1,0:T(2,128)} %neighbors_h.3, s32[2,128]{1,0:T(2,128)} %pivots_h.1, bf16[2,128,512]{2,1,0:T(8,128)(2,1)} %interp_h.1, ...), custom_call_target="tpu_custom_call" | custom-call | tf_op jit(solution)/shard_map/early/pallas_call | solution.py:188
  6.5 3.0 %collective-permute-start = (bf16[4,128,128]{2,1,0:T(8,128)(2,1)S(1)}, bf16[4,128,128]{2,1,0:T(8,128)(2,1)S(1)}, u32[]{:S(2)}, u32[]{:S(2)}) collective-permute-start(bf16[4,128,128]{2,1,0:T(8,128)(2,1)S(1)} %get-tuple-element.13), channel_id=1, source_target_pairs={{0,4},{4,0},{8,12},{12,8},{16,20},{20,16},{24,28},{28,24},{1,5},{5... | collective-permute-start | bytes 393224 | tf_op jit(solution)/shard_map/ppermute | solution.py:169
  9.5 1.6 %collective-permute-start.1 = (bf16[4,128,128]{2,1,0:T(8,128)(2,1)S(1)}, bf16[4,128,128]{2,1,0:T(8,128)(2,1)S(1)}, u32[]{:S(2)}, u32[]{:S(2)}) collective-permute-start(bf16[4,128,128]{2,1,0:T(8,128)(2,1)S(1)} %get-tuple-element.14), channel_id=1, source_target_pairs={{0,8},{4,12},{8,0},{12,4},{16,24},{20,28},{24,16},{28,20},{1,9},{5... | collective-permute-start | bytes 393224 | tf_op jit(solution)/shard_map/ppermute | solution.py:169
  11.1 0.0 collective-permute-start.2
  11.1 0.0 copy-start.2
  11.1 0.0 copy-start
  11.1 3.8 %late.1 = (bf16[2,128,128]{2,1,0:T(8,128)(2,1)S(1)}, bf16[2,128,128]{2,1,0:T(8,128)(2,1)S(1)}) custom-call(s32[2,14]{1,0:T(2,128)} %neighbors_h.3, bf16[2,14,128,512]{3,2,1,0:T(8,128)(2,1)} %back_h.3, bf16[2,14,512,128]{3,2,1,0:T(8,128)(2,1)} %near_h.3, bf16[2,512,512]{2,1,0:T(8,128)(2,1)S(1)} %get-tuple-element.11.elim_v), custom_call_target="tpu_custom_call" | custom-call | tf_op jit(solution)/shard_map/late/pallas_call | solution.py:211
  14.9 0.0 copy-done.2
  15.0 0.0 collective-permute-done
  15.0 0.9 %collective-permute-done.1 = bf16[4,128,128]{2,1,0:T(8,128)(2,1)S(1)} collective-permute-done((bf16[4,128,128]{2,1,0:T(8,128)(2,1)S(1)}, bf16[4,128,128]{2,1,0:T(8,128)(2,1)S(1)}, u32[]{:S(2)}, u32[]{:S(2)}) %collective-permute-start.1) | collective-permute-done | bytes 131104 | tf_op jit(solution)/shard_map/ppermute | solution.py:169
  15.9 1.2 %collective-permute-done.2 = bf16[4,128,128]{2,1,0:T(8,128)(2,1)S(1)} collective-permute-done((bf16[4,128,128]{2,1,0:T(8,128)(2,1)S(1)}, bf16[4,128,128]{2,1,0:T(8,128)(2,1)S(1)}, u32[]{:S(2)}, u32[]{:S(2)}) %collective-permute-start.2) | collective-permute-done | bytes 131104 | tf_op jit(solution)/shard_map/ppermute | solution.py:169
  17.1 2.8 %collective-permute-start.3 = (bf16[2,128,128]{2,1,0:T(8,128)(2,1)S(1)}, bf16[2,128,128]{2,1,0:T(8,128)(2,1)S(1)}, u32[]{:S(2)}, u32[]{:S(2)}) collective-permute-start(bf16[2,128,128]{2,1,0:T(8,128)(2,1)S(1)} %fusion), channel_id=1, source_target_pairs={{0,16},{4,20},{8,24},{12,28},{16,0},{20,4},{24,8},{28,12},{1,17},{... | collective-permute-start | bytes 196616 | tf_op jit(solution)/shard_map/ppermute | solution.py:169
  20.0 0.0 copy-done.1
  20.0 0.1 iota_compare_fusion
  20.1 2.3 %collective-permute-done.3 = bf16[2,128,128]{2,1,0:T(8,128)(2,1)S(1)} collective-permute-done((bf16[2,128,128]{2,1,0:T(8,128)(2,1)S(1)}, bf16[2,128,128]{2,1,0:T(8,128)(2,1)S(1)}, u32[]{:S(2)}, u32[]{:S(2)}) %collective-permute-start.3) | collective-permute-done | bytes 65568 | tf_op jit(solution)/shard_map/ppermute | solution.py:169
  22.4 0.0 copy-done
  22.4 0.2 select_reduce_fusion.5
  22.6 1.8 %collective-permute-start.5 = (bf16[2,128,128]{2,1,0:T(8,128)(2,1)S(1)}, bf16[2,128,128]{2,1,0:T(8,128)(2,1)S(1)}, u32[]{:S(2)}, u32[]{:S(2)}) collective-permute-start(bf16[2,128,128]{2,1,0:T(8,128)(2,1)S(1)} %pad_maximum_fusion.1), channel_id=1, source_target_pairs={{0,2},{1,3},{2,0},{3,1},{4,6},{5,7},{6,4},{7,5},{8,10},{9,11},{10,... | collective-permute-start | bytes 196616 | tf_op jit(solution)/shard_map/ppermute | solution.py:169
  24.3 0.1 collective-permute-start.6
  24.4 0.5 %collective-permute-start.4 = (bf16[2,128,128]{2,1,0:T(8,128)(2,1)S(1)}, bf16[2,128,128]{2,1,0:T(8,128)(2,1)S(1)}, u32[]{:S(2)}, u32[]{:S(2)}) collective-permute-start(bf16[2,128,128]{2,1,0:T(8,128)(2,1)S(1)} %pad_maximum_fusion), channel_id=1, source_target_pairs={{0,1},{1,0},{2,3},{3,2},{4,5},{5,4},{6,7},{7,6},{8,9},{9,8},{10,11... | collective-permute-start | bytes 196616 | tf_op jit(solution)/shard_map/ppermute | solution.py:169
  24.9 2.0 %collective-permute-done.5 = bf16[2,128,128]{2,1,0:T(8,128)(2,1)S(1)} collective-permute-done((bf16[2,128,128]{2,1,0:T(8,128)(2,1)S(1)}, bf16[2,128,128]{2,1,0:T(8,128)(2,1)S(1)}, u32[]{:S(2)}, u32[]{:S(2)}) %collective-permute-start.5) | collective-permute-done | bytes 65568 | tf_op jit(solution)/shard_map/ppermute | solution.py:169
  26.9 1.4 %collective-permute-done.6 = bf16[2,128,128]{2,1,0:T(8,128)(2,1)S(1)} collective-permute-done((bf16[2,128,128]{2,1,0:T(8,128)(2,1)S(1)}, bf16[2,128,128]{2,1,0:T(8,128)(2,1)S(1)}, u32[]{:S(2)}, u32[]{:S(2)}) %collective-permute-start.6) | collective-permute-done | bytes 65568 | tf_op jit(solution)/shard_map/ppermute | solution.py:169
  28.3 0.0 collective-permute-done.4
  28.3 0.7 %fusion.5 = f32[2,128,128]{2,1,0:T(8,128)} fusion(f32[1,128,128]{2,1,0:T(8,128)S(1)} %bitcast.20, f32[1,128,128]{2,1,0:T(8,128)S(1)} %bitcast.21, bf16[2,128,128]{2,1,0:T(8,128)(2,1)S(1)} %collective-permute-done.6, bf16[2,128,128]{2,1,0:T(8,128)(2,1)S(1)} %collective-permute-done.5, bf16[2,128,128]{2,1,0:T(8,128)(2,1)S(1)} %collective-permute-done.4), kind=kLoop, calls=%fused_computation.12 | loop fusion | flops 229376 | bytes 458752 | tf_op jit(solution)/shard_map/add | solution.py:245
  (10 shorter events, 0.1 us)
Async XLA Ops:
  6.5 8.5 %collective-permute-start = (bf16[4,128,128]{2,1,0:T(8,128)(2,1)S(1)}, bf16[4,128,128]{2,1,0:T(8,128)(2,1)S(1)}, u32[]{:S(2)}, u32[]{:S(2)}) collective-permute-start(bf16[4,128,128]{2,1,0:T(8,128)(2,1)S(1)} %get-tuple-element.13), channel_id=1, source_target_pairs={{0,4},{4,0},{8,12},{12,8},{16,20},{20,16},{24,28},{28,24},{1,5},{5... | collective-permute-start | bytes 393224 | tf_op jit(solution)/shard_map/ppermute | solution.py:169
  9.5 6.4 %collective-permute-start.1 = (bf16[4,128,128]{2,1,0:T(8,128)(2,1)S(1)}, bf16[4,128,128]{2,1,0:T(8,128)(2,1)S(1)}, u32[]{:S(2)}, u32[]{:S(2)}) collective-permute-start(bf16[4,128,128]{2,1,0:T(8,128)(2,1)S(1)} %get-tuple-element.14), channel_id=1, source_target_pairs={{0,8},{4,12},{8,0},{12,4},{16,24},{20,28},{24,16},{28,20},{1,9},{5... | collective-permute-start | bytes 393224 | tf_op jit(solution)/shard_map/ppermute | solution.py:169
  11.1 6.0 %collective-permute-start.2 = (bf16[4,128,128]{2,1,0:T(8,128)(2,1)S(1)}, bf16[4,128,128]{2,1,0:T(8,128)(2,1)S(1)}, u32[]{:S(2)}, u32[]{:S(2)}) collective-permute-start(bf16[4,128,128]{2,1,0:T(8,128)(2,1)S(1)} %get-tuple-element.15), channel_id=1, source_target_pairs={{0,12},{4,8},{8,4},{12,0},{16,28},{20,24},{24,20},{28,16},{1,13},{... | collective-permute-start | bytes 393224 | tf_op jit(solution)/shard_map/ppermute | solution.py:169
  11.1 3.8 %copy-start.2 = (s32[2]{0:T(128)S(1)}, s32[2]{0:T(128)}, u32[]{:S(2)}) copy-start(s32[2]{0:T(128)} %param.17) | copy-start | bytes 28
  11.1 8.9 %copy-start.1 = (s32[2]{0:T(128)S(1)}, s32[2]{0:T(128)}, u32[]{:S(2)}) copy-start(s32[2]{0:T(128)} %ranks_h.1) | copy-start | bytes 28
  11.1 11.3 %copy-start = (f32[2,128,128]{2,1,0:T(8,128)S(1)}, f32[2,128,128]{2,1,0:T(8,128)}, u32[]{:S(2)}) copy-start(f32[2,128,128]{2,1,0:T(8,128)} %param.9) | copy-start | bytes 393220
  17.1 5.2 %collective-permute-start.3 = (bf16[2,128,128]{2,1,0:T(8,128)(2,1)S(1)}, bf16[2,128,128]{2,1,0:T(8,128)(2,1)S(1)}, u32[]{:S(2)}, u32[]{:S(2)}) collective-permute-start(bf16[2,128,128]{2,1,0:T(8,128)(2,1)S(1)} %fusion), channel_id=1, source_target_pairs={{0,16},{4,20},{8,24},{12,28},{16,0},{20,4},{24,8},{28,12},{1,17},{... | collective-permute-start | bytes 196616 | tf_op jit(solution)/shard_map/ppermute | solution.py:169
  22.6 4.3 %collective-permute-start.5 = (bf16[2,128,128]{2,1,0:T(8,128)(2,1)S(1)}, bf16[2,128,128]{2,1,0:T(8,128)(2,1)S(1)}, u32[]{:S(2)}, u32[]{:S(2)}) collective-permute-start(bf16[2,128,128]{2,1,0:T(8,128)(2,1)S(1)} %pad_maximum_fusion.1), channel_id=1, source_target_pairs={{0,2},{1,3},{2,0},{3,1},{4,6},{5,7},{6,4},{7,5},{8,10},{9,11},{10,... | collective-permute-start | bytes 196616 | tf_op jit(solution)/shard_map/ppermute | solution.py:169
  24.3 4.0 %collective-permute-start.6 = (bf16[2,128,128]{2,1,0:T(8,128)(2,1)S(1)}, bf16[2,128,128]{2,1,0:T(8,128)(2,1)S(1)}, u32[]{:S(2)}, u32[]{:S(2)}) collective-permute-start(bf16[2,128,128]{2,1,0:T(8,128)(2,1)S(1)} %pad_maximum_fusion.2), channel_id=1, source_target_pairs={{0,3},{1,2},{2,1},{3,0},{4,7},{5,6},{6,5},{7,4},{8,11},{9,10},{10,... | collective-permute-start | bytes 196616 | tf_op jit(solution)/shard_map/ppermute | solution.py:169
  24.4 3.9 %collective-permute-start.4 = (bf16[2,128,128]{2,1,0:T(8,128)(2,1)S(1)}, bf16[2,128,128]{2,1,0:T(8,128)(2,1)S(1)}, u32[]{:S(2)}, u32[]{:S(2)}) collective-permute-start(bf16[2,128,128]{2,1,0:T(8,128)(2,1)S(1)} %pad_maximum_fusion), channel_id=1, source_target_pairs={{0,1},{1,0},{2,3},{3,2},{4,5},{5,4},{6,7},{7,6},{8,9},{9,8},{10,11... | collective-permute-start | bytes 196616 | tf_op jit(solution)/shard_map/ppermute | solution.py:169

commit v4 on v3

--- a/solution.py
+++ b/solution.py
@@ -18,8 +18,8 @@
     return jnp.dot(a, b, preferred_element_type=jnp.float32)
 
 
-def eliminator_of(interp, redinv, pivot_row, rank):
-    width, points = interp.shape
+def selections(pivot_row, rank, points):
+    width = pivot_row.shape[1]
     pivot_col = jnp.transpose(jnp.broadcast_to(pivot_row, (8, width)))[:, :1]
     slot = lax.broadcasted_iota(jnp.int32, (width, points), 0)
     point = lax.broadcasted_iota(jnp.int32, (width, points), 1)
@@ -29,13 +29,24 @@
     point_t = lax.broadcasted_iota(jnp.int32, (points, width), 0)
     select_t = jnp.where((point_t == pivot_row) & (slot_t < rank), 1.0, 0.0)
     redundant_col = jnp.max(select_t, axis=1, keepdims=True) < 0.5
-    coefficients = jnp.where((slot < rank) & redundant_row, interp, jnp.zeros_like(interp))
-    half_skel = (-nt(redinv, coefficients)).astype(jnp.bfloat16)
-    spread = nn(half_skel, select.astype(jnp.bfloat16)).astype(jnp.bfloat16)
-    halfway = jnp.where(redundant_row, redinv, spread)
-    elim_skel = (-nn(coefficients, halfway)).astype(jnp.bfloat16)
-    spread = nn(select_t.astype(jnp.bfloat16), elim_skel).astype(jnp.bfloat16)
-    return jnp.where(redundant_col, halfway, spread)
+    return select.astype(jnp.bfloat16), select_t.astype(jnp.bfloat16), redundant_row, redundant_col
+
+
+def eliminators_of(interps, redinvs, chosen, ranks):
+    boxes = range(len(ranks))
+    bf16 = jnp.bfloat16
+    select, select_t, redundant_row, redundant_col = zip(*chosen)
+    slot = lax.broadcasted_iota(jnp.int32, interps[0].shape, 0)
+    coefficients = [
+        jnp.where((slot < ranks[b]) & redundant_row[b], interps[b], jnp.zeros_like(interps[b]))
+        for b in boxes
+    ]
+    half_skel = [(-nt(redinvs[b], coefficients[b])).astype(bf16) for b in boxes]
+    spread = [nn(half_skel[b], select[b]).astype(bf16) for b in boxes]
+    halfway = [jnp.where(redundant_row[b], redinvs[b], spread[b]) for b in boxes]
+    elim_skel = [(-nn(coefficients[b], halfway[b])).astype(bf16) for b in boxes]
+    spread = [nn(select_t[b], elim_skel[b]).astype(bf16) for b in boxes]
+    return [jnp.where(redundant_col[b], halfway[b], spread[b]) for b in boxes]
 
 
 def fill_table(table, neighbors, box_dev, near_count, lane_count, slots):
@@ -48,25 +59,6 @@
             target = neighbors[b, n]
             row = target // (box_dev * lane_count)
             table[b, (row ^ me) * box_dev + target % box_dev] = n
-
-
-def slot_updates(table, slots, elims, back_v, near_v, lifted_v, near_count, group, store, ready=None):
-    box_dev, _, width, _ = back_v.shape
-    for first in range(0, len(slots), group):
-        these = slots[first : first + group]
-        for b in range(box_dev):
-            rows = jnp.concatenate([back_v[b, table[b, u]] for u in these], axis=0)
-            lifted_v[b, pl.ds(0, len(these) * width)] = nn(rows, elims[b][...]).astype(jnp.bfloat16)
-        if ready is not None and first == 0:
-            ready()
-        for i, u in enumerate(these):
-            total = None
-            for b in range(box_dev):
-                if u != b:
-                    n = jnp.minimum(table[b, u], near_count - 1)
-                    term = nn(lifted_v[b, pl.ds(i * width, width)], near_v[b, n])
-                    total = term if total is None else total + term
-            store(first + i, (-total).astype(jnp.bfloat16))
 
 
 def early_kernel(sizes, early):
@@ -99,29 +91,54 @@
         for b in range(box_dev):
             copies[b][0].start()
             copies[b][1].start()
+
+        def lift(b):
+            for first in range(0, len(early), 16):
+                some = early[first : first + 16]
+                rows = jnp.concatenate([back_v[b, table[b, u]] for u in some], axis=0)
+                span = pl.ds(first * width, len(some) * width)
+                lifted_v[b, span] = nn(rows, elim_v[b]).astype(jnp.bfloat16)
+
+        def update(i):
+            total = None
+            for b in range(box_dev):
+                n = jnp.minimum(table[b, early[i]], near_count - 1)
+                term = nn(lifted_v[b, pl.ds(i * width, width)], near_v[b, n])
+                total = term if total is None else total + term
+            outs[i // group][i % group] = (-total).astype(jnp.bfloat16)
+
+        def start(j, boxes):
+            for b in boxes:
+                copies[b][j].start()
+
+        def wait(j, boxes):
+            for b in boxes:
+                copies[b][j].wait()
+
+        boxes = range(box_dev)
         for b in range(box_dev):
             back_v[b, near_count] = jnp.zeros((width, points), jnp.bfloat16)
         for copy in heads:
             copy.wait()
+        wait(0, boxes[:1])
+        wait(1, boxes[:1])
+        start(2, boxes)
         fill_table(table, neighbors, box_dev, near_count, lane_count, slots)
-        elims = []
-        for b in range(box_dev):
-            copies[b][0].wait()
-            copies[b][1].wait()
-            if b == 0:
-                for j in (2, 3):
-                    for c in range(box_dev):
-                        copies[c][j].start()
-        for b in range(box_dev):
-            elim_v[b] = eliminator_of(interp_v[b], redinv_v[b], pivots[pl.ds(b, 1), :], ranks[b])
-            elims.append(elim_v.at[b])
-        for b in range(box_dev):
-            copies[b][2].wait()
-
-        def store(i, block):
-            outs[i // group][i % group] = block
-
-        slot_updates(table, early, elims, back_v, near_v, lifted_v, near_count, group, store, lambda: [copies[b][3].wait() for b in range(box_dev)])
+        wait(0, boxes[1:])
+        wait(1, boxes[1:])
+        start(3, boxes)
+        chosen = [selections(pivots[pl.ds(b, 1), :], ranks[b], points) for b in boxes]
+        made = eliminators_of(
+            [interp_v[b] for b in boxes], [redinv_v[b] for b in boxes], chosen, [ranks[b] for b in boxes]
+        )
+        for b in boxes:
+            elim_v[b] = made[b]
+        wait(2, boxes)
+        for b in boxes:
+            lift(b)
+        wait(3, boxes)
+        for i in range(len(early)):
+            update(i)
 
     return kernel
 
@@ -141,8 +158,12 @@
         for b in range(box_dev):
             for i, u in enumerate(late):
                 n = jnp.minimum(table[b, u], near_count - 1)
-                copies.append(pltpu.make_async_copy(back_h.at[b, n], back_v.at[b, i], sems.at[0, b, i]))
-                copies.append(pltpu.make_async_copy(near_h.at[b, n], near_v.at[b, i], sems.at[1, b, i]))
+                for side, (source, target) in enumerate(((back_h, back_v), (near_h, near_v))):
+                    copies.append(
+                        pltpu.make_async_copy(
+                            source.at[b, n], target.at[b, i], sems.at[side, b, i]
+                        )
+                    )
         for copy in copies:
             copy.start()
         for copy in copies:
@@ -184,7 +205,7 @@
     hbm = pl.BlockSpec(memory_space=pltpu.HBM)
     vmem = pl.BlockSpec(memory_space=pltpu.VMEM)
     table = pltpu.SMEM((box_dev, gx_count * box_dev), jnp.int32)
-    params = pltpu.CompilerParams(vmem_limit_bytes=24 * 1024 * 1024)
+    params = pltpu.CompilerParams(vmem_limit_bytes=48 * 1024 * 1024)
     *early, elim = pl.pallas_call(
         early_kernel(sizes, slots_of(early_k)),
         out_shape=[jax.ShapeDtypeStruct((group, width, width), bf16)] * len(peers)
@@ -199,7 +220,7 @@
             pltpu.VMEM(redinv.shape, bf16),
             pltpu.VMEM((box_dev, near_count + 1, width, points), bf16),
             pltpu.VMEM(near.shape, bf16),
-            pltpu.VMEM((box_dev, group * width, points), bf16),
+            pltpu.VMEM((box_dev, len(early_k) * box_dev * width, points), bf16),
             table,
             pltpu.SemaphoreType.DMA((3,)),
             pltpu.SemaphoreType.DMA((box_dev, 4)),
@@ -259,4 +280,6 @@
         P(split, None),
         P(split),
     )
-    return jax.shard_map(layer, mesh=mesh, in_specs=placed, out_specs=P(split, None, None), check_vma=False)
+    return jax.shard_map(
+        layer, mesh=mesh, in_specs=placed, out_specs=P(split, None, None), check_vma=False
+    )

time: 29.2 us -> 28.8 us (0.986)
  Pallas kernels: 10.3 us -> 9.89 us
    pallas_call x1, Pallas kernels: 6.48 us -> 6.08 us  [layer(): pl.pallas_call(early_kernel(sizes, slots_of(early_k)), out_shape=[jax.Sha...]
where the time goes in v4:
time: 28.8 us; the launch traced here: 28.6 us
  Pallas kernels  9.89 us (34%)
  starting transfers between devices  9.75 us (34%)
  waiting for transfers between devices  7.76 us (27%)
  other arithmetic  1.07 us (4%)
    ppermute x7, starting transfers between devices, swap(): return lax.ppermute(value, axis, [(a, a ^ k) for a in range(size)])  9.75 us
    ppermute x7, waiting for transfers between devices, swap(): return lax.ppermute(value, axis, [(a, a ^ k) for a in range(size)])  7.76 us
    pallas_call x1, Pallas kernels, layer(): pl.pallas_call(early_kernel(sizes, slots_of(early_k)), out_shape=[jax.Sha...  6.08 us
    pallas_call x1, Pallas kernels, layer(): pl.pallas_call(late_kernel(sizes, slots_of(late_k)), out_shape=[jax.Shape...  3.81 us
    add x1, other arithmetic, layer(): result = placed if result is None else result + placed  0.69 us
  transfers between devices with their start and end apart: 7, of which 5 were waited for; matrix products, arithmetic and copies ran while one was open for 1% of the time, Pallas kernels for 13%

profile of v4, /device:TPU:0, one launch (start us, length us, event | category | flops | bytes accessed | tf_op | source)
XLA Modules:
  0.0 28.6 jit_solution(2569262314907058129)
XLA Ops:
  0.0 6.1 %early.1 = (bf16[4,128,128]{2,1,0:T(8,128)(2,1)S(1)}, bf16[4,128,128]{2,1,0:T(8,128)(2,1)S(1)}, bf16[4,128,128]{2,1,0:T(8,128)(2,1)S(1)}, bf16[2,512,512]{2,1,0:T(8,128)(2,1)S(1)}) custom-call(s32[2]{0:T(128)} %ranks_h.1, s32[2,14]{1,0:T(2,128)} %neighbors_h.3, s32[2,128]{1,0:T(2,128)} %pivots_h.1, bf16[2,128,512]{2,1,0:T(8,128)(2,1)} %interp_h.1, ...), custom_call_target="tpu_custom_call" | custom-call | tf_op jit(solution)/shard_map/early/pallas_call | solution.py:209
  6.1 3.0 %collective-permute-start = (bf16[4,128,128]{2,1,0:T(8,128)(2,1)S(1)}, bf16[4,128,128]{2,1,0:T(8,128)(2,1)S(1)}, u32[]{:S(2)}, u32[]{:S(2)}) collective-permute-start(bf16[4,128,128]{2,1,0:T(8,128)(2,1)S(1)} %get-tuple-element.13), channel_id=1, source_target_pairs={{0,4},{4,0},{8,12},{12,8},{16,20},{20,16},{24,28},{28,24},{1,5},{5... | collective-permute-start | bytes 393224 | tf_op jit(solution)/shard_map/ppermute | solution.py:190
  9.1 1.6 %collective-permute-start.1 = (bf16[4,128,128]{2,1,0:T(8,128)(2,1)S(1)}, bf16[4,128,128]{2,1,0:T(8,128)(2,1)S(1)}, u32[]{:S(2)}, u32[]{:S(2)}) collective-permute-start(bf16[4,128,128]{2,1,0:T(8,128)(2,1)S(1)} %get-tuple-element.14), channel_id=1, source_target_pairs={{0,8},{4,12},{8,0},{12,4},{16,24},{20,28},{24,16},{28,20},{1,9},{5... | collective-permute-start | bytes 393224 | tf_op jit(solution)/shard_map/ppermute | solution.py:190
  10.7 0.0 collective-permute-start.2
  10.7 0.0 copy-start.2
  10.7 0.0 copy-start.1
  10.7 3.8 %late.1 = (bf16[2,128,128]{2,1,0:T(8,128)(2,1)S(1)}, bf16[2,128,128]{2,1,0:T(8,128)(2,1)S(1)}) custom-call(s32[2,14]{1,0:T(2,128)} %neighbors_h.3, bf16[2,14,128,512]{3,2,1,0:T(8,128)(2,1)} %back_h.3, bf16[2,14,512,128]{3,2,1,0:T(8,128)(2,1)} %near_h.3, bf16[2,512,512]{2,1,0:T(8,128)(2,1)S(1)} %get-tuple-element.11.elim_v), custom_call_target="tpu_custom_call" | custom-call | tf_op jit(solution)/shard_map/late/pallas_call | solution.py:232
  14.5 0.0 copy-done.2
  14.6 0.0 collective-permute-done
  14.6 0.9 %collective-permute-done.1 = bf16[4,128,128]{2,1,0:T(8,128)(2,1)S(1)} collective-permute-done((bf16[4,128,128]{2,1,0:T(8,128)(2,1)S(1)}, bf16[4,128,128]{2,1,0:T(8,128)(2,1)S(1)}, u32[]{:S(2)}, u32[]{:S(2)}) %collective-permute-start.1) | collective-permute-done | bytes 131104 | tf_op jit(solution)/shard_map/ppermute | solution.py:190
  15.5 1.2 %collective-permute-done.2 = bf16[4,128,128]{2,1,0:T(8,128)(2,1)S(1)} collective-permute-done((bf16[4,128,128]{2,1,0:T(8,128)(2,1)S(1)}, bf16[4,128,128]{2,1,0:T(8,128)(2,1)S(1)}, u32[]{:S(2)}, u32[]{:S(2)}) %collective-permute-start.2) | collective-permute-done | bytes 131104 | tf_op jit(solution)/shard_map/ppermute | solution.py:190
  16.8 2.8 %collective-permute-start.3 = (bf16[2,128,128]{2,1,0:T(8,128)(2,1)S(1)}, bf16[2,128,128]{2,1,0:T(8,128)(2,1)S(1)}, u32[]{:S(2)}, u32[]{:S(2)}) collective-permute-start(bf16[2,128,128]{2,1,0:T(8,128)(2,1)S(1)} %fusion), channel_id=1, source_target_pairs={{0,16},{4,20},{8,24},{12,28},{16,0},{20,4},{24,8},{28,12},{1,17},{... | collective-permute-start | bytes 196616 | tf_op jit(solution)/shard_map/ppermute | solution.py:190
  19.6 0.0 copy-done.1
  19.6 0.1 iota_compare_fusion
  19.7 2.3 %collective-permute-done.3 = bf16[2,128,128]{2,1,0:T(8,128)(2,1)S(1)} collective-permute-done((bf16[2,128,128]{2,1,0:T(8,128)(2,1)S(1)}, bf16[2,128,128]{2,1,0:T(8,128)(2,1)S(1)}, u32[]{:S(2)}, u32[]{:S(2)}) %collective-permute-start.3) | collective-permute-done | bytes 65568 | tf_op jit(solution)/shard_map/ppermute | solution.py:190
  22.0 0.0 copy-done
  22.0 0.2 select_reduce_fusion.5
  22.2 1.8 %collective-permute-start.5 = (bf16[2,128,128]{2,1,0:T(8,128)(2,1)S(1)}, bf16[2,128,128]{2,1,0:T(8,128)(2,1)S(1)}, u32[]{:S(2)}, u32[]{:S(2)}) collective-permute-start(bf16[2,128,128]{2,1,0:T(8,128)(2,1)S(1)} %pad_maximum_fusion.1), channel_id=1, source_target_pairs={{0,2},{1,3},{2,0},{3,1},{4,6},{5,7},{6,4},{7,5},{8,10},{9,11},{10,... | collective-permute-start | bytes 196616 | tf_op jit(solution)/shard_map/ppermute | solution.py:190
  23.9 0.1 collective-permute-start.6
  24.0 0.5 %collective-permute-start.4 = (bf16[2,128,128]{2,1,0:T(8,128)(2,1)S(1)}, bf16[2,128,128]{2,1,0:T(8,128)(2,1)S(1)}, u32[]{:S(2)}, u32[]{:S(2)}) collective-permute-start(bf16[2,128,128]{2,1,0:T(8,128)(2,1)S(1)} %pad_maximum_fusion), channel_id=1, source_target_pairs={{0,1},{1,0},{2,3},{3,2},{4,5},{5,4},{6,7},{7,6},{8,9},{9,8},{10,11... | collective-permute-start | bytes 196616 | tf_op jit(solution)/shard_map/ppermute | solution.py:190
  24.5 2.0 %collective-permute-done.5 = bf16[2,128,128]{2,1,0:T(8,128)(2,1)S(1)} collective-permute-done((bf16[2,128,128]{2,1,0:T(8,128)(2,1)S(1)}, bf16[2,128,128]{2,1,0:T(8,128)(2,1)S(1)}, u32[]{:S(2)}, u32[]{:S(2)}) %collective-permute-start.5) | collective-permute-done | bytes 65568 | tf_op jit(solution)/shard_map/ppermute | solution.py:190
  26.5 1.4 %collective-permute-done.6 = bf16[2,128,128]{2,1,0:T(8,128)(2,1)S(1)} collective-permute-done((bf16[2,128,128]{2,1,0:T(8,128)(2,1)S(1)}, bf16[2,128,128]{2,1,0:T(8,128)(2,1)S(1)}, u32[]{:S(2)}, u32[]{:S(2)}) %collective-permute-start.6) | collective-permute-done | bytes 65568 | tf_op jit(solution)/shard_map/ppermute | solution.py:190
  27.9 0.0 collective-permute-done.4
  27.9 0.7 %fusion.5 = f32[2,128,128]{2,1,0:T(8,128)} fusion(f32[1,128,128]{2,1,0:T(8,128)S(1)} %bitcast.20, f32[1,128,128]{2,1,0:T(8,128)S(1)} %bitcast.21, bf16[2,128,128]{2,1,0:T(8,128)(2,1)S(1)} %collective-permute-done.6, bf16[2,128,128]{2,1,0:T(8,128)(2,1)S(1)} %collective-permute-done.5, bf16[2,128,128]{2,1,0:T(8,128)(2,1)S(1)} %collective-permute-done.4), kind=kLoop, calls=%fused_computation.12 | loop fusion | flops 229376 | bytes 458752 | tf_op jit(solution)/shard_map/add | solution.py:266
  (10 shorter events, 0.1 us)
Async XLA Ops:
  6.1 8.5 %collective-permute-start = (bf16[4,128,128]{2,1,0:T(8,128)(2,1)S(1)}, bf16[4,128,128]{2,1,0:T(8,128)(2,1)S(1)}, u32[]{:S(2)}, u32[]{:S(2)}) collective-permute-start(bf16[4,128,128]{2,1,0:T(8,128)(2,1)S(1)} %get-tuple-element.13), channel_id=1, source_target_pairs={{0,4},{4,0},{8,12},{12,8},{16,20},{20,16},{24,28},{28,24},{1,5},{5... | collective-permute-start | bytes 393224 | tf_op jit(solution)/shard_map/ppermute | solution.py:190
  9.1 6.4 %collective-permute-start.1 = (bf16[4,128,128]{2,1,0:T(8,128)(2,1)S(1)}, bf16[4,128,128]{2,1,0:T(8,128)(2,1)S(1)}, u32[]{:S(2)}, u32[]{:S(2)}) collective-permute-start(bf16[4,128,128]{2,1,0:T(8,128)(2,1)S(1)} %get-tuple-element.14), channel_id=1, source_target_pairs={{0,8},{4,12},{8,0},{12,4},{16,24},{20,28},{24,16},{28,20},{1,9},{5... | collective-permute-start | bytes 393224 | tf_op jit(solution)/shard_map/ppermute | solution.py:190
  10.7 6.0 %collective-permute-start.2 = (bf16[4,128,128]{2,1,0:T(8,128)(2,1)S(1)}, bf16[4,128,128]{2,1,0:T(8,128)(2,1)S(1)}, u32[]{:S(2)}, u32[]{:S(2)}) collective-permute-start(bf16[4,128,128]{2,1,0:T(8,128)(2,1)S(1)} %get-tuple-element.15), channel_id=1, source_target_pairs={{0,12},{4,8},{8,4},{12,0},{16,28},{20,24},{24,20},{28,16},{1,13},{... | collective-permute-start | bytes 393224 | tf_op jit(solution)/shard_map/ppermute | solution.py:190
  10.7 3.8 %copy-start.2 = (s32[2]{0:T(128)S(1)}, s32[2]{0:T(128)}, u32[]{:S(2)}) copy-start(s32[2]{0:T(128)} %param.17) | copy-start | bytes 28
  10.7 8.9 %copy-start.1 = (s32[2]{0:T(128)S(1)}, s32[2]{0:T(128)}, u32[]{:S(2)}) copy-start(s32[2]{0:T(128)} %ranks_h.1) | copy-start | bytes 28
  10.7 11.3 %copy-start = (f32[2,128,128]{2,1,0:T(8,128)S(1)}, f32[2,128,128]{2,1,0:T(8,128)}, u32[]{:S(2)}) copy-start(f32[2,128,128]{2,1,0:T(8,128)} %param.9) | copy-start | bytes 393220
  16.8 5.2 %collective-permute-start.3 = (bf16[2,128,128]{2,1,0:T(8,128)(2,1)S(1)}, bf16[2,128,128]{2,1,0:T(8,128)(2,1)S(1)}, u32[]{:S(2)}, u32[]{:S(2)}) collective-permute-start(bf16[2,128,128]{2,1,0:T(8,128)(2,1)S(1)} %fusion), channel_id=1, source_target_pairs={{0,16},{4,20},{8,24},{12,28},{16,0},{20,4},{24,8},{28,12},{1,17},{... | collective-permute-start | bytes 196616 | tf_op jit(solution)/shard_map/ppermute | solution.py:190
  22.2 4.3 %collective-permute-start.5 = (bf16[2,128,128]{2,1,0:T(8,128)(2,1)S(1)}, bf16[2,128,128]{2,1,0:T(8,128)(2,1)S(1)}, u32[]{:S(2)}, u32[]{:S(2)}) collective-permute-start(bf16[2,128,128]{2,1,0:T(8,128)(2,1)S(1)} %pad_maximum_fusion.1), channel_id=1, source_target_pairs={{0,2},{1,3},{2,0},{3,1},{4,6},{5,7},{6,4},{7,5},{8,10},{9,11},{10,... | collective-permute-start | bytes 196616 | tf_op jit(solution)/shard_map/ppermute | solution.py:190
  23.9 4.0 %collective-permute-start.6 = (bf16[2,128,128]{2,1,0:T(8,128)(2,1)S(1)}, bf16[2,128,128]{2,1,0:T(8,128)(2,1)S(1)}, u32[]{:S(2)}, u32[]{:S(2)}) collective-permute-start(bf16[2,128,128]{2,1,0:T(8,128)(2,1)S(1)} %pad_maximum_fusion.2), channel_id=1, source_target_pairs={{0,3},{1,2},{2,1},{3,0},{4,7},{5,6},{6,5},{7,4},{8,11},{9,10},{10,... | collective-permute-start | bytes 196616 | tf_op jit(solution)/shard_map/ppermute | solution.py:190
  24.0 3.9 %collective-permute-start.4 = (bf16[2,128,128]{2,1,0:T(8,128)(2,1)S(1)}, bf16[2,128,128]{2,1,0:T(8,128)(2,1)S(1)}, u32[]{:S(2)}, u32[]{:S(2)}) collective-permute-start(bf16[2,128,128]{2,1,0:T(8,128)(2,1)S(1)} %pad_maximum_fusion), channel_id=1, source_target_pairs={{0,1},{1,0},{2,3},{3,2},{4,5},{5,4},{6,7},{7,6},{8,9},{9,8},{10,11... | collective-permute-start | bytes 196616 | tf_op jit(solution)/shard_map/ppermute | solution.py:190

commit v5 on v4

--- a/solution.py
+++ b/solution.py
@@ -19,34 +19,38 @@
 
 
 def selections(pivot_row, rank, points):
+    bf16 = jnp.bfloat16
     width = pivot_row.shape[1]
     pivot_col = jnp.transpose(jnp.broadcast_to(pivot_row, (8, width)))[:, :1]
     slot = lax.broadcasted_iota(jnp.int32, (width, points), 0)
     point = lax.broadcasted_iota(jnp.int32, (width, points), 1)
     select = jnp.where((point == pivot_col) & (slot < rank), 1.0, 0.0)
-    redundant_row = jnp.sum(select, axis=0, keepdims=True) < 0.5
+    redundant_row = 1.0 - jnp.sum(select, axis=0, keepdims=True)
     slot_t = lax.broadcasted_iota(jnp.int32, (points, width), 1)
     point_t = lax.broadcasted_iota(jnp.int32, (points, width), 0)
-    select_t = jnp.where((point_t == pivot_row) & (slot_t < rank), 1.0, 0.0)
-    redundant_col = jnp.max(select_t, axis=1, keepdims=True) < 0.5
-    return select.astype(jnp.bfloat16), select_t.astype(jnp.bfloat16), redundant_row, redundant_col
-
-
-def eliminators_of(interps, redinvs, chosen, ranks):
-    boxes = range(len(ranks))
+    minus_t = jnp.where((point_t == pivot_row) & (slot_t < rank), -1.0, 0.0)
+    redundant_col = 1.0 + jnp.min(minus_t, axis=1, keepdims=True)
+    alive = jnp.where(slot[:, :1] < rank, -1.0, 0.0)
+    return (
+        select.astype(bf16),
+        minus_t.astype(bf16),
+        redundant_row.astype(bf16),
+        redundant_col.astype(bf16),
+        alive.astype(bf16),
+    )
+
+
+def eliminators_of(interps, redinvs, chosen):
+    boxes = range(len(interps))
     bf16 = jnp.bfloat16
-    select, select_t, redundant_row, redundant_col = zip(*chosen)
-    slot = lax.broadcasted_iota(jnp.int32, interps[0].shape, 0)
-    coefficients = [
-        jnp.where((slot < ranks[b]) & redundant_row[b], interps[b], jnp.zeros_like(interps[b]))
-        for b in boxes
-    ]
-    half_skel = [(-nt(redinvs[b], coefficients[b])).astype(bf16) for b in boxes]
+    select, minus_t, redundant_row, redundant_col, alive = zip(*chosen)
+    minus_c = [interps[b] * alive[b] * redundant_row[b] for b in boxes]
+    half_skel = [nt(redinvs[b], minus_c[b]).astype(bf16) for b in boxes]
     spread = [nn(half_skel[b], select[b]).astype(bf16) for b in boxes]
-    halfway = [jnp.where(redundant_row[b], redinvs[b], spread[b]) for b in boxes]
-    elim_skel = [(-nn(coefficients[b], halfway[b])).astype(bf16) for b in boxes]
-    spread = [nn(select_t[b], elim_skel[b]).astype(bf16) for b in boxes]
-    return [jnp.where(redundant_col[b], halfway[b], spread[b]) for b in boxes]
+    halfway = [redinvs[b] * redundant_row[b] + spread[b] for b in boxes]
+    elim_skel = [nn(minus_c[b], halfway[b]).astype(bf16) for b in boxes]
+    spread = [nn(minus_t[b], elim_skel[b]).astype(bf16) for b in boxes]
+    return [spread[b] - halfway[b] * redundant_col[b] for b in boxes]
 
 
 def fill_table(table, neighbors, box_dev, near_count, lane_count, slots):
@@ -105,7 +109,7 @@
                 n = jnp.minimum(table[b, early[i]], near_count - 1)
                 term = nn(lifted_v[b, pl.ds(i * width, width)], near_v[b, n])
                 total = term if total is None else total + term
-            outs[i // group][i % group] = (-total).astype(jnp.bfloat16)
+            outs[i // group][i % group] = total.astype(jnp.bfloat16)
 
         def start(j, boxes):
             for b in boxes:
@@ -129,12 +133,12 @@
         start(3, boxes)
         chosen = [selections(pivots[pl.ds(b, 1), :], ranks[b], points) for b in boxes]
         made = eliminators_of(
-            [interp_v[b] for b in boxes], [redinv_v[b] for b in boxes], chosen, [ranks[b] for b in boxes]
+            [interp_v[b] for b in boxes], [redinv_v[b] for b in boxes], chosen
         )
         for b in boxes:
             elim_v[b] = made[b]
-        wait(2, boxes)
         for b in boxes:
+            wait(2, [b])
             lift(b)
         wait(3, boxes)
         for i in range(len(early)):
@@ -177,7 +181,7 @@
             for b in range(box_dev):
                 term = nn(lifted[b][i * width : (i + 1) * width], near_v[b, i])
                 total += jnp.where(table[b, u] < near_count, term, 0.0)
-            outs[i // box_dev][i % box_dev] = (-total).astype(jnp.bfloat16)
+            outs[i // box_dev][i % box_dev] = total.astype(jnp.bfloat16)
 
     return kernel
 

time: 28.8 us -> 28.6 us (level)
  no operation moved by 1% of the time
where the time goes in v5:
time: 28.6 us; the launch traced here: 28.4 us
  starting transfers between devices  9.76 us (34%)
  Pallas kernels  9.67 us (34%)
  waiting for transfers between devices  7.76 us (27%)
  other arithmetic  1.07 us (4%)
    ppermute x7, starting transfers between devices, swap(): return lax.ppermute(value, axis, [(a, a ^ k) for a in range(size)])  9.76 us
    ppermute x7, waiting for transfers between devices, swap(): return lax.ppermute(value, axis, [(a, a ^ k) for a in range(size)])  7.76 us
    pallas_call x1, Pallas kernels, layer(): pl.pallas_call(early_kernel(sizes, slots_of(early_k)), out_shape=[jax.Sha...  5.86 us
    pallas_call x1, Pallas kernels, layer(): pl.pallas_call(late_kernel(sizes, slots_of(late_k)), out_shape=[jax.Shape...  3.81 us
    add x1, other arithmetic, layer(): result = placed if result is None else result + placed  0.69 us
  transfers between devices with their start and end apart: 7, of which 5 were waited for; matrix products, arithmetic and copies ran while one was open for 1% of the time, Pallas kernels for 13%

profile of v5, /device:TPU:0, one launch (start us, length us, event | category | flops | bytes accessed | tf_op | source)
XLA Modules:
  0.0 28.4 jit_solution(16241900602679457692)
XLA Ops:
  0.0 5.9 %early.1 = (bf16[4,128,128]{2,1,0:T(8,128)(2,1)S(1)}, bf16[4,128,128]{2,1,0:T(8,128)(2,1)S(1)}, bf16[4,128,128]{2,1,0:T(8,128)(2,1)S(1)}, bf16[2,512,512]{2,1,0:T(8,128)(2,1)S(1)}) custom-call(s32[2]{0:T(128)} %ranks_h.1, s32[2,14]{1,0:T(2,128)} %neighbors_h.3, s32[2,128]{1,0:T(2,128)} %pivots_h.1, bf16[2,128,512]{2,1,0:T(8,128)(2,1)} %interp_h.1, ...), custom_call_target="tpu_custom_call" | custom-call | tf_op jit(solution)/shard_map/early/pallas_call | solution.py:213
  5.9 3.0 %collective-permute-start = (bf16[4,128,128]{2,1,0:T(8,128)(2,1)S(1)}, bf16[4,128,128]{2,1,0:T(8,128)(2,1)S(1)}, u32[]{:S(2)}, u32[]{:S(2)}) collective-permute-start(bf16[4,128,128]{2,1,0:T(8,128)(2,1)S(1)} %get-tuple-element.13), channel_id=1, source_target_pairs={{0,4},{4,0},{8,12},{12,8},{16,20},{20,16},{24,28},{28,24},{1,5},{5... | collective-permute-start | bytes 393224 | tf_op jit(solution)/shard_map/ppermute | solution.py:194
  8.9 1.6 %collective-permute-start.1 = (bf16[4,128,128]{2,1,0:T(8,128)(2,1)S(1)}, bf16[4,128,128]{2,1,0:T(8,128)(2,1)S(1)}, u32[]{:S(2)}, u32[]{:S(2)}) collective-permute-start(bf16[4,128,128]{2,1,0:T(8,128)(2,1)S(1)} %get-tuple-element.14), channel_id=1, source_target_pairs={{0,8},{4,12},{8,0},{12,4},{16,24},{20,28},{24,16},{28,20},{1,9},{5... | collective-permute-start | bytes 393224 | tf_op jit(solution)/shard_map/ppermute | solution.py:194
  10.5 0.0 collective-permute-start.2
  10.5 0.0 copy-start.2
  10.5 0.0 copy-start.1
  10.5 3.8 %late.1 = (bf16[2,128,128]{2,1,0:T(8,128)(2,1)S(1)}, bf16[2,128,128]{2,1,0:T(8,128)(2,1)S(1)}) custom-call(s32[2,14]{1,0:T(2,128)} %neighbors_h.3, bf16[2,14,128,512]{3,2,1,0:T(8,128)(2,1)} %back_h.3, bf16[2,14,512,128]{3,2,1,0:T(8,128)(2,1)} %near_h.3, bf16[2,512,512]{2,1,0:T(8,128)(2,1)S(1)} %get-tuple-element.11.elim_v), custom_call_target="tpu_custom_call" | custom-call | tf_op jit(solution)/shard_map/late/pallas_call | solution.py:236
  14.3 0.0 copy-done.2
  14.4 0.0 collective-permute-done
  14.4 0.9 %collective-permute-done.1 = bf16[4,128,128]{2,1,0:T(8,128)(2,1)S(1)} collective-permute-done((bf16[4,128,128]{2,1,0:T(8,128)(2,1)S(1)}, bf16[4,128,128]{2,1,0:T(8,128)(2,1)S(1)}, u32[]{:S(2)}, u32[]{:S(2)}) %collective-permute-start.1) | collective-permute-done | bytes 131104 | tf_op jit(solution)/shard_map/ppermute | solution.py:194
  15.3 1.2 %collective-permute-done.2 = bf16[4,128,128]{2,1,0:T(8,128)(2,1)S(1)} collective-permute-done((bf16[4,128,128]{2,1,0:T(8,128)(2,1)S(1)}, bf16[4,128,128]{2,1,0:T(8,128)(2,1)S(1)}, u32[]{:S(2)}, u32[]{:S(2)}) %collective-permute-start.2) | collective-permute-done | bytes 131104 | tf_op jit(solution)/shard_map/ppermute | solution.py:194
  16.5 2.8 %collective-permute-start.3 = (bf16[2,128,128]{2,1,0:T(8,128)(2,1)S(1)}, bf16[2,128,128]{2,1,0:T(8,128)(2,1)S(1)}, u32[]{:S(2)}, u32[]{:S(2)}) collective-permute-start(bf16[2,128,128]{2,1,0:T(8,128)(2,1)S(1)} %fusion), channel_id=1, source_target_pairs={{0,16},{4,20},{8,24},{12,28},{16,0},{20,4},{24,8},{28,12},{1,17},{... | collective-permute-start | bytes 196616 | tf_op jit(solution)/shard_map/ppermute | solution.py:194
  19.4 0.0 copy-done.1
  19.4 0.1 iota_compare_fusion
  19.4 2.3 %collective-permute-done.3 = bf16[2,128,128]{2,1,0:T(8,128)(2,1)S(1)} collective-permute-done((bf16[2,128,128]{2,1,0:T(8,128)(2,1)S(1)}, bf16[2,128,128]{2,1,0:T(8,128)(2,1)S(1)}, u32[]{:S(2)}, u32[]{:S(2)}) %collective-permute-start.3) | collective-permute-done | bytes 65568 | tf_op jit(solution)/shard_map/ppermute | solution.py:194
  21.8 0.0 copy-done
  21.8 0.2 select_reduce_fusion.5
  22.0 1.8 %collective-permute-start.5 = (bf16[2,128,128]{2,1,0:T(8,128)(2,1)S(1)}, bf16[2,128,128]{2,1,0:T(8,128)(2,1)S(1)}, u32[]{:S(2)}, u32[]{:S(2)}) collective-permute-start(bf16[2,128,128]{2,1,0:T(8,128)(2,1)S(1)} %pad_maximum_fusion.1), channel_id=1, source_target_pairs={{0,2},{1,3},{2,0},{3,1},{4,6},{5,7},{6,4},{7,5},{8,10},{9,11},{10,... | collective-permute-start | bytes 196616 | tf_op jit(solution)/shard_map/ppermute | solution.py:194
  23.7 0.1 collective-permute-start.6
  23.8 0.5 %collective-permute-start.4 = (bf16[2,128,128]{2,1,0:T(8,128)(2,1)S(1)}, bf16[2,128,128]{2,1,0:T(8,128)(2,1)S(1)}, u32[]{:S(2)}, u32[]{:S(2)}) collective-permute-start(bf16[2,128,128]{2,1,0:T(8,128)(2,1)S(1)} %pad_maximum_fusion), channel_id=1, source_target_pairs={{0,1},{1,0},{2,3},{3,2},{4,5},{5,4},{6,7},{7,6},{8,9},{9,8},{10,11... | collective-permute-start | bytes 196616 | tf_op jit(solution)/shard_map/ppermute | solution.py:194
  24.3 2.0 %collective-permute-done.5 = bf16[2,128,128]{2,1,0:T(8,128)(2,1)S(1)} collective-permute-done((bf16[2,128,128]{2,1,0:T(8,128)(2,1)S(1)}, bf16[2,128,128]{2,1,0:T(8,128)(2,1)S(1)}, u32[]{:S(2)}, u32[]{:S(2)}) %collective-permute-start.5) | collective-permute-done | bytes 65568 | tf_op jit(solution)/shard_map/ppermute | solution.py:194
  26.3 1.4 %collective-permute-done.6 = bf16[2,128,128]{2,1,0:T(8,128)(2,1)S(1)} collective-permute-done((bf16[2,128,128]{2,1,0:T(8,128)(2,1)S(1)}, bf16[2,128,128]{2,1,0:T(8,128)(2,1)S(1)}, u32[]{:S(2)}, u32[]{:S(2)}) %collective-permute-start.6) | collective-permute-done | bytes 65568 | tf_op jit(solution)/shard_map/ppermute | solution.py:194
  27.7 0.0 collective-permute-done.4
  27.7 0.7 %fusion.5 = f32[2,128,128]{2,1,0:T(8,128)} fusion(f32[1,128,128]{2,1,0:T(8,128)S(1)} %bitcast.20, f32[1,128,128]{2,1,0:T(8,128)S(1)} %bitcast.21, bf16[2,128,128]{2,1,0:T(8,128)(2,1)S(1)} %collective-permute-done.6, bf16[2,128,128]{2,1,0:T(8,128)(2,1)S(1)} %collective-permute-done.5, bf16[2,128,128]{2,1,0:T(8,128)(2,1)S(1)} %collective-permute-done.4), kind=kLoop, calls=%fused_computation.12 | loop fusion | flops 229376 | bytes 458752 | tf_op jit(solution)/shard_map/add | solution.py:270
  (10 shorter events, 0.1 us)
Async XLA Ops:
  5.9 8.5 %collective-permute-start = (bf16[4,128,128]{2,1,0:T(8,128)(2,1)S(1)}, bf16[4,128,128]{2,1,0:T(8,128)(2,1)S(1)}, u32[]{:S(2)}, u32[]{:S(2)}) collective-permute-start(bf16[4,128,128]{2,1,0:T(8,128)(2,1)S(1)} %get-tuple-element.13), channel_id=1, source_target_pairs={{0,4},{4,0},{8,12},{12,8},{16,20},{20,16},{24,28},{28,24},{1,5},{5... | collective-permute-start | bytes 393224 | tf_op jit(solution)/shard_map/ppermute | solution.py:194
  8.9 6.4 %collective-permute-start.1 = (bf16[4,128,128]{2,1,0:T(8,128)(2,1)S(1)}, bf16[4,128,128]{2,1,0:T(8,128)(2,1)S(1)}, u32[]{:S(2)}, u32[]{:S(2)}) collective-permute-start(bf16[4,128,128]{2,1,0:T(8,128)(2,1)S(1)} %get-tuple-element.14), channel_id=1, source_target_pairs={{0,8},{4,12},{8,0},{12,4},{16,24},{20,28},{24,16},{28,20},{1,9},{5... | collective-permute-start | bytes 393224 | tf_op jit(solution)/shard_map/ppermute | solution.py:194
  10.5 6.0 %collective-permute-start.2 = (bf16[4,128,128]{2,1,0:T(8,128)(2,1)S(1)}, bf16[4,128,128]{2,1,0:T(8,128)(2,1)S(1)}, u32[]{:S(2)}, u32[]{:S(2)}) collective-permute-start(bf16[4,128,128]{2,1,0:T(8,128)(2,1)S(1)} %get-tuple-element.15), channel_id=1, source_target_pairs={{0,12},{4,8},{8,4},{12,0},{16,28},{20,24},{24,20},{28,16},{1,13},{... | collective-permute-start | bytes 393224 | tf_op jit(solution)/shard_map/ppermute | solution.py:194
  10.5 3.8 %copy-start.2 = (s32[2]{0:T(128)S(1)}, s32[2]{0:T(128)}, u32[]{:S(2)}) copy-start(s32[2]{0:T(128)} %param.17) | copy-start | bytes 28
  10.5 8.9 %copy-start.1 = (s32[2]{0:T(128)S(1)}, s32[2]{0:T(128)}, u32[]{:S(2)}) copy-start(s32[2]{0:T(128)} %ranks_h.1) | copy-start | bytes 28
  10.5 11.3 %copy-start = (f32[2,128,128]{2,1,0:T(8,128)S(1)}, f32[2,128,128]{2,1,0:T(8,128)}, u32[]{:S(2)}) copy-start(f32[2,128,128]{2,1,0:T(8,128)} %param.9) | copy-start | bytes 393220
  16.5 5.2 %collective-permute-start.3 = (bf16[2,128,128]{2,1,0:T(8,128)(2,1)S(1)}, bf16[2,128,128]{2,1,0:T(8,128)(2,1)S(1)}, u32[]{:S(2)}, u32[]{:S(2)}) collective-permute-start(bf16[2,128,128]{2,1,0:T(8,128)(2,1)S(1)} %fusion), channel_id=1, source_target_pairs={{0,16},{4,20},{8,24},{12,28},{16,0},{20,4},{24,8},{28,12},{1,17},{... | collective-permute-start | bytes 196616 | tf_op jit(solution)/shard_map/ppermute | solution.py:194
  22.0 4.3 %collective-permute-start.5 = (bf16[2,128,128]{2,1,0:T(8,128)(2,1)S(1)}, bf16[2,128,128]{2,1,0:T(8,128)(2,1)S(1)}, u32[]{:S(2)}, u32[]{:S(2)}) collective-permute-start(bf16[2,128,128]{2,1,0:T(8,128)(2,1)S(1)} %pad_maximum_fusion.1), channel_id=1, source_target_pairs={{0,2},{1,3},{2,0},{3,1},{4,6},{5,7},{6,4},{7,5},{8,10},{9,11},{10,... | collective-permute-start | bytes 196616 | tf_op jit(solution)/shard_map/ppermute | solution.py:194
  23.7 4.0 %collective-permute-start.6 = (bf16[2,128,128]{2,1,0:T(8,128)(2,1)S(1)}, bf16[2,128,128]{2,1,0:T(8,128)(2,1)S(1)}, u32[]{:S(2)}, u32[]{:S(2)}) collective-permute-start(bf16[2,128,128]{2,1,0:T(8,128)(2,1)S(1)} %pad_maximum_fusion.2), channel_id=1, source_target_pairs={{0,3},{1,2},{2,1},{3,0},{4,7},{5,6},{6,5},{7,4},{8,11},{9,10},{10,... | collective-permute-start | bytes 196616 | tf_op jit(solution)/shard_map/ppermute | solution.py:194
  23.8 3.9 %collective-permute-start.4 = (bf16[2,128,128]{2,1,0:T(8,128)(2,1)S(1)}, bf16[2,128,128]{2,1,0:T(8,128)(2,1)S(1)}, u32[]{:S(2)}, u32[]{:S(2)}) collective-permute-start(bf16[2,128,128]{2,1,0:T(8,128)(2,1)S(1)} %pad_maximum_fusion), channel_id=1, source_target_pairs={{0,1},{1,0},{2,3},{3,2},{4,5},{5,4},{6,7},{7,6},{8,9},{9,8},{10,11... | collective-permute-start | bytes 196616 | tf_op jit(solution)/shard_map/ppermute | solution.py:194
